TPU v7x, 32 devices: a whole 2x2x4 slice. The times are simulated.
32 devices in a mesh: ctx: 16 (over z, y, core), fsdp: 2 (over x).
Axes of the slice: x: 2, y: 2, z: 4, core: 2. Of those that a mesh axis runs over, the one named last changes fastest.
Arguments:
- tokens: bfloat16 [2, 4096, 1024], P('fsdp', 'ctx'), may hold values from -6 to 6
- segments: int32 [2, 4096], P('fsdp'), may hold values from 0 to 7, never falling along the last dimension, each value on 1 to 3072 neighbouring positions
- w_query: bfloat16 [1024, 1024], P('fsdp'), may hold values from -0.1875 to 0.1875
- w_key: bfloat16 [1024, 1024], P('fsdp'), may hold values from -0.1875 to 0.1875
- w_value: bfloat16 [1024, 1024], P('fsdp'), may hold values from -0.1875 to 0.1875
- w_out: bfloat16 [1024, 1024], P('fsdp'), may hold values from -0.75 to 0.75
- b_query: bfloat16 [1024], P('fsdp'), may hold values from -3 to 3
- b_value: bfloat16 [1024], P('fsdp'), may hold values from -3 to 3
- b_out: bfloat16 [1024], P('fsdp'), may hold values from -3 to 3
- gain_one: bfloat16 [1024], P('fsdp'), may hold values from 0.099609375 to 1.8984375
- shift_one: bfloat16 [1024], P('fsdp'), may hold values from -3 to 3
- w_up: bfloat16 [1024, 4096], P('fsdp'), may hold values from -0.1875 to 0.1875
- b_up: bfloat16 [4096], P('fsdp'), may hold values from -3 to 3
- w_down: bfloat16 [4096, 1024], P('fsdp'), may hold values from -0.09375 to 0.09375
- b_down: bfloat16 [1024], P('fsdp'), may hold values from -3 to 3
- gain_two: bfloat16 [1024], P('fsdp'), may hold values from 0.099609375 to 1.8984375
- shift_two: bfloat16 [1024], P('fsdp'), may hold values from -3 to 3
- cotangent: bfloat16 [2, 4096, 1024], P('fsdp', 'ctx'), may hold values from -6 to 6
Outputs:
- layer_out: bfloat16 [2, 4096, 1024], P('fsdp', 'ctx')
- token_grad: bfloat16 [2, 4096, 1024], P('fsdp', 'ctx')
- grad_w_query: float32 [1024, 1024], P('fsdp')
- grad_w_key: float32 [1024, 1024], P('fsdp')
- grad_w_value: float32 [1024, 1024], P('fsdp')
- grad_w_out: float32 [1024, 1024], P('fsdp')
- grad_b_query: float32 [1024], P('fsdp')
- grad_b_value: float32 [1024], P('fsdp')
- grad_b_out: float32 [1024], P('fsdp')
- grad_gain_one: float32 [1024], P('fsdp')
- grad_shift_one: float32 [1024], P('fsdp')
- grad_w_up: float32 [1024, 4096], P('fsdp')
- grad_b_up: float32 [4096], P('fsdp')
- grad_w_down: float32 [4096, 1024], P('fsdp')
- grad_b_down: float32 [1024], P('fsdp')
- grad_gain_two: float32 [1024], P('fsdp')
- grad_shift_two: float32 [1024], P('fsdp')
Inputs may be any that keep to these rules, and one draw needn't show every extreme that they name: `segments`: within each sequence the document numbers start at 0, never fall and use every number up to 7; no document has more than 3072 tokens, and one in each sequence has exactly 3072.
All inputs are finite; a program needn't handle non-finite values.
Results may differ from a plain program's by a relative error of at most 0.013.
Values may be sent and summed in bfloat16 or wider, within the bound.
No kernel may reach another device: no remote copies, remote signals or barrier semaphores. Data moves between devices by JAX's collectives and lax.ppermute only.
A program may use at most 256 MiB of HBM per device.

v0:
```python
import math

import jax
import jax.numpy as jnp
from jax import lax
from jax.sharding import PartitionSpec as P

HEADS = 16


def layer_norm(hidden, gain, shift):
    mean = jnp.mean(hidden, axis=-1, keepdims=True)
    centred = hidden - mean
    variance = jnp.mean(centred * centred, axis=-1, keepdims=True)
    return centred * lax.rsqrt(variance + 1e-05) * gain + shift


def gelu_exact(value):
    return jax.nn.gelu(value, approximate=False)


def dense(left, right):
    return jnp.dot(left, right, preferred_element_type=jnp.float32)


def left_product(left, right):
    return jnp.einsum("ti,tj->ij", left, right, preferred_element_type=jnp.float32)


def right_product(left, right):
    return jnp.einsum("ti,ji->tj", left, right, preferred_element_type=jnp.float32)


def to_heads(rows_data, seqs, count, heads):
    return rows_data.reshape(seqs, count, heads, -1).transpose(2, 0, 1, 3)


def from_heads(head_data):
    return head_data.transpose(1, 2, 0, 3).reshape(head_data.shape[1] * head_data.shape[2], -1)


def body(
    tokens,
    segments,
    w_query,
    w_key,
    w_value,
    w_out,
    b_query,
    b_value,
    b_out,
    gain_one,
    shift_one,
    w_up,
    b_up,
    w_down,
    b_down,
    gain_two,
    shift_two,
    cotangent,
):
    seqs, block, width = tokens.shape
    heads = HEADS
    scale = 1.0 / math.sqrt(width // heads)
    start = lax.axis_index("ctx") * block
    wq, wk, wv, wo, bq, bv, bo, gain1, shift1 = (
        lax.all_gather(w_query, "fsdp", axis=0, tiled=True),
        lax.all_gather(w_key, "fsdp", axis=0, tiled=True),
        lax.all_gather(w_value, "fsdp", axis=0, tiled=True),
        lax.all_gather(w_out, "fsdp", axis=0, tiled=True),
        lax.all_gather(b_query, "fsdp", axis=0, tiled=True),
        lax.all_gather(b_value, "fsdp", axis=0, tiled=True),
        lax.all_gather(b_out, "fsdp", axis=0, tiled=True),
        lax.all_gather(gain_one, "fsdp", axis=0, tiled=True),
        lax.all_gather(shift_one, "fsdp", axis=0, tiled=True),
    )
    wu, bu, wd, bd, gain2, shift2 = (
        lax.all_gather(w_up, "fsdp", axis=0, tiled=True),
        lax.all_gather(b_up, "fsdp", axis=0, tiled=True),
        lax.all_gather(w_down, "fsdp", axis=0, tiled=True),
        lax.all_gather(b_down, "fsdp", axis=0, tiled=True),
        lax.all_gather(gain_two, "fsdp", axis=0, tiled=True),
        lax.all_gather(shift_two, "fsdp", axis=0, tiled=True),
    )
    inputs = tokens.reshape(seqs * block, width)
    queries = (dense(inputs, wq) + bq.astype(jnp.float32)).astype(jnp.bfloat16)
    keys = dense(inputs, wk).astype(jnp.bfloat16)
    values = (dense(inputs, wv) + bv.astype(jnp.float32)).astype(jnp.bfloat16)
    query_heads = to_heads(queries, seqs, block, heads)
    key_local = to_heads(keys, seqs, block, heads)
    value_local = to_heads(values, seqs, block, heads)
    key_all, value_all = (
        lax.all_gather(key_local, "ctx", axis=2, tiled=True),
        lax.all_gather(value_local, "ctx", axis=2, tiled=True),
    )
    own_seg = lax.dynamic_slice_in_dim(segments, start, block, 1)
    same = own_seg[:, :, None] == segments[:, None, :]

    def scores_of(query_part, key_part):
        raw = (
            jnp.einsum("sre,sle->srl", query_part, key_part, preferred_element_type=jnp.float32)
            * scale
        )
        return jnp.where(same, raw, -1e30)

    def forward_head(carry, item):
        query_part, key_part, value_part = item
        scores = scores_of(query_part, key_part)
        peak = jnp.max(scores, axis=-1, keepdims=True)
        expo = jnp.exp(scores - peak)
        total = jnp.sum(expo, axis=-1, keepdims=True)
        probs = (expo / total).astype(jnp.bfloat16)
        result = jnp.einsum("srl,sle->sre", probs, value_part, preferred_element_type=jnp.float32)
        return (carry, (result, peak[..., 0] + jnp.log(total[..., 0])))

    unused, (attended, log_total) = lax.scan(
        forward_head, jnp.zeros((), jnp.float32), (query_heads, key_all, value_all)
    )
    attended = from_heads(attended).astype(jnp.bfloat16)
    branch = dense(attended, wo) + bo.astype(jnp.float32)
    first, first_pull = jax.vjp(
        layer_norm,
        inputs.astype(jnp.float32) + branch,
        gain1.astype(jnp.float32),
        shift1.astype(jnp.float32),
    )
    first_low = first.astype(jnp.bfloat16)
    hidden_pre = dense(first_low, wu) + bu.astype(jnp.float32)
    active, active_pull = jax.vjp(gelu_exact, hidden_pre)
    active_low = active.astype(jnp.bfloat16)
    second = dense(active_low, wd) + bd.astype(jnp.float32)
    output, out_pull = jax.vjp(
        layer_norm, first + second, gain2.astype(jnp.float32), shift2.astype(jnp.float32)
    )
    d_out = cotangent.reshape(seqs * block, width).astype(jnp.float32)
    d_second, grad_gain_two, grad_shift_two = out_pull(d_out)
    grad_b_down = jnp.sum(d_second, axis=0)
    d_second_low = d_second.astype(jnp.bfloat16)
    grad_w_down = left_product(active_low, d_second_low)
    (d_hidden,) = active_pull(right_product(d_second_low, wd))
    grad_b_up = jnp.sum(d_hidden, axis=0)
    d_hidden_low = d_hidden.astype(jnp.bfloat16)
    grad_w_up = left_product(first_low, d_hidden_low)
    d_first = d_second + right_product(d_hidden_low, wu)
    d_branch, grad_gain_one, grad_shift_one = first_pull(d_first)
    grad_b_out = jnp.sum(d_branch, axis=0)
    d_branch_low = d_branch.astype(jnp.bfloat16)
    grad_w_out = left_product(attended, d_branch_low)
    d_attended = to_heads(right_product(d_branch_low, wo).astype(jnp.bfloat16), seqs, block, heads)
    key_back, value_back = (
        lax.all_gather(key_local, "ctx", axis=2, tiled=True),
        lax.all_gather(value_local, "ctx", axis=2, tiled=True),
    )

    def query_head(carry, item):
        query_part, key_part, value_part, lse_part, grad_part = item
        probs = jnp.exp(scores_of(query_part, key_part) - lse_part[..., None])
        d_probs = jnp.einsum(
            "sre,sle->srl", grad_part, value_part, preferred_element_type=jnp.float32
        )
        row_sum = jnp.sum(probs * d_probs, axis=-1)
        d_scores = (probs * (d_probs - row_sum[..., None])).astype(jnp.bfloat16)
        d_q = (
            jnp.einsum("srl,sle->sre", d_scores, key_part, preferred_element_type=jnp.float32)
            * scale
        )
        return (carry, (d_q, row_sum))

    unused, (d_query, row_sums) = lax.scan(
        query_head,
        jnp.zeros((), jnp.float32),
        (query_heads, key_back, value_back, log_total, d_attended),
    )
    query_every, grad_every = (
        lax.all_gather(query_heads, "ctx", axis=2, tiled=True),
        lax.all_gather(d_attended, "ctx", axis=2, tiled=True),
    )
    lse_every, sums_every = (
        lax.all_gather(log_total, "ctx", axis=2, tiled=True),
        lax.all_gather(row_sums, "ctx", axis=2, tiled=True),
    )
    same_owner = segments[:, :, None] == own_seg[:, None, :]

    def owner_head(carry, item):
        query_part, grad_part, lse_part, sum_part, key_part, value_part = item
        raw = (
            jnp.einsum("sre,sle->srl", query_part, key_part, preferred_element_type=jnp.float32)
            * scale
        )
        probs = jnp.exp(jnp.where(same_owner, raw, -1e30) - lse_part[..., None])
        d_probs = jnp.einsum(
            "sre,sle->srl", grad_part, value_part, preferred_element_type=jnp.float32
        )
        d_scores = (probs * (d_probs - sum_part[..., None])).astype(jnp.bfloat16)
        d_k = (
            jnp.einsum("srl,sre->sle", d_scores, query_part, preferred_element_type=jnp.float32)
            * scale
        )
        d_v = jnp.einsum(
            "srl,sre->sle",
            probs.astype(jnp.bfloat16),
            grad_part,
            preferred_element_type=jnp.float32,
        )
        return (carry, (d_k, d_v))

    unused, (d_key, d_value) = lax.scan(
        owner_head,
        jnp.zeros((), jnp.float32),
        (query_every, grad_every, lse_every, sums_every, key_local, value_local),
    )
    d_query = from_heads(d_query)
    d_key = from_heads(d_key)
    d_value = from_heads(d_value)
    grad_b_query = jnp.sum(d_query, axis=0)
    grad_b_value = jnp.sum(d_value, axis=0)
    query_low = d_query.astype(jnp.bfloat16)
    key_low = d_key.astype(jnp.bfloat16)
    value_low = d_value.astype(jnp.bfloat16)
    grad_w_query = left_product(inputs, query_low)
    grad_w_key = left_product(inputs, key_low)
    grad_w_value = left_product(inputs, value_low)
    token_grad = (
        d_branch
        + right_product(query_low, wq)
        + right_product(key_low, wk)
        + right_product(value_low, wv)
    )
    shards = (
        lax.psum_scatter(grad_w_query, "fsdp", scatter_dimension=0, tiled=True),
        lax.psum_scatter(grad_w_key, "fsdp", scatter_dimension=0, tiled=True),
        lax.psum_scatter(grad_w_value, "fsdp", scatter_dimension=0, tiled=True),
        lax.psum_scatter(grad_w_out, "fsdp", scatter_dimension=0, tiled=True),
        lax.psum_scatter(grad_b_query, "fsdp", scatter_dimension=0, tiled=True),
        lax.psum_scatter(grad_b_value, "fsdp", scatter_dimension=0, tiled=True),
        lax.psum_scatter(grad_b_out, "fsdp", scatter_dimension=0, tiled=True),
        lax.psum_scatter(grad_gain_one, "fsdp", scatter_dimension=0, tiled=True),
        lax.psum_scatter(grad_shift_one, "fsdp", scatter_dimension=0, tiled=True),
        lax.psum_scatter(grad_w_up, "fsdp", scatter_dimension=0, tiled=True),
        lax.psum_scatter(grad_b_up, "fsdp", scatter_dimension=0, tiled=True),
        lax.psum_scatter(grad_w_down, "fsdp", scatter_dimension=0, tiled=True),
        lax.psum_scatter(grad_b_down, "fsdp", scatter_dimension=0, tiled=True),
        lax.psum_scatter(grad_gain_two, "fsdp", scatter_dimension=0, tiled=True),
        lax.psum_scatter(grad_shift_two, "fsdp", scatter_dimension=0, tiled=True),
    )
    totals = lax.psum(
        (
            shards[0],
            shards[1],
            shards[2],
            shards[3],
            shards[4],
            shards[5],
            shards[6],
            shards[7],
            shards[8],
            shards[9],
            shards[10],
            shards[11],
            shards[12],
            shards[13],
            shards[14],
        ),
        "ctx",
    )
    layer_out = output.reshape(seqs, block, width).astype(jnp.bfloat16)
    token_out = token_grad.reshape(seqs, block, width).astype(jnp.bfloat16)
    return (layer_out, token_out) + tuple(totals)


def solution(mesh):
    placed = (
        P("fsdp", "ctx", None),
        P("fsdp", None),
        P("fsdp", None),
        P("fsdp", None),
        P("fsdp", None),
        P("fsdp", None),
        P("fsdp"),
        P("fsdp"),
        P("fsdp"),
        P("fsdp"),
        P("fsdp"),
        P("fsdp", None),
        P("fsdp"),
        P("fsdp", None),
        P("fsdp"),
        P("fsdp"),
        P("fsdp"),
        P("fsdp", "ctx", None),
    )
    return jax.shard_map(
        body,
        mesh=mesh,
        in_specs=placed,
        out_specs=(
            P("fsdp", "ctx", None),
            P("fsdp", "ctx", None),
            P("fsdp", None),
            P("fsdp", None),
            P("fsdp", None),
            P("fsdp", None),
            P("fsdp"),
            P("fsdp"),
            P("fsdp"),
            P("fsdp"),
            P("fsdp"),
            P("fsdp", None),
            P("fsdp"),
            P("fsdp", None),
            P("fsdp"),
            P("fsdp"),
            P("fsdp"),
        ),
        check_vma=False,
    )
```

profile of v0, /device:TPU:0, one launch (start us, length us, event | category | flops | bytes accessed | tf_op | source)
XLA Modules:
  0.0 1867.9 jit_solution(7085819776734267962)
XLA Ops:
  10.1 5.3 all-gather.1
  15.4 30.0 %all-gather.25.cloned.1.call-done = bf16[1024,1024]{1,0:T(8,128)(2,1)} async-done(((bf16[512,1024]{1,0:T(8,128)(2,1)}), bf16[1024,1024]{1,0:T(8,128)(2,1)}) %all-gather.25.cloned.1.call-update) | async-done | bytes 2097168 | tf_op jit(solution)/shard_map/all_gather | solution.py:69
  49.0 31.1 %all-gather.21.cloned.1.call-done = bf16[1024,1024]{1,0:T(8,128)(2,1)} async-done(((bf16[512,1024]{1,0:T(8,128)(2,1)}), bf16[1024,1024]{1,0:T(8,128)(2,1)}) %all-gather.21.cloned.1.call-update) | async-done | bytes 2097168 | tf_op jit(solution)/shard_map/all_gather | solution.py:68
  85.7 4.4 all-gather
  90.1 4.5 all-gather.2
  94.7 4.5 all-gather.3
  99.2 4.5 all-gather.4
  103.8 4.6 all_gather.77
  108.4 4.5 all-gather.5
  112.9 4.4 all-gather.6
  117.3 4.4 all-gather.7
  125.7 69.1 %all-gather.27.cloned.1.call-done = bf16[16,1,4096,64]{2,3,0,1:T(8,128)(2,1)} async-done(((bf16[16,1,256,64]{2,3,0,1:T(8,128)(2,1)}), bf16[16,1,4096,64]{2,3,0,1:T(8,128)(2,1)}) %all-gather.27.cloned.1.call-update) | async-done | bytes 8388624 | tf_op jit(solution)/shard_map/all_gather | solution.py:94
  194.8 15.7 copy.65
  210.5 62.2 %all-gather.23.cloned.1.call-done = bf16[16,1,4096,64]{2,3,0,1:T(8,128)(2,1)} async-done(((bf16[16,1,256,64]{2,3,0,1:T(8,128)(2,1)}), bf16[16,1,4096,64]{2,3,0,1:T(8,128)(2,1)}) %all-gather.23.cloned.1.call-update) | async-done | bytes 8388624 | tf_op jit(solution)/shard_map/all_gather | solution.py:93
  272.7 15.8 copy.64
  288.5 82.7 %while.39 = (s32[]{:T(128)}, bf16[16,1,256,64]{2,3,1,0:T(8,128)(2,1)S(1)}, f32[16,1,256]{2,1,0:T(1,128)S(1)}, bf16[16,1,256,64]{3,2,1,0:T(8,128)(2,1)S(1)}, bf16...) while((s32[]{:T(128)}, ...), condition=%wide.region_3.4_spmd.clone, body=%wide.region_0.3_spmd.clone.sunk | while | flops 277872384 | bytes 14840929 | solution.py:116
  374.9 36.0 %all-gather.31.cloned.1.call-done = bf16[1024,4096]{1,0:T(8,128)(2,1)} async-done(((bf16[512,4096]{1,0:T(8,128)(2,1)}), bf16[1024,4096]{1,0:T(8,128)(2,1)}) %all-gather.31.cloned.1.call-update) | async-done | bytes 8388624 | tf_op jit(solution)/shard_map/all_gather | solution.py:78
  410.9 16.2 multiply_convert_fusion.8
  427.1 89.4 %all-gather.33.cloned.1.call-done = bf16[4096,1024]{1,0:T(8,128)(2,1)} async-done(((bf16[2048,1024]{1,0:T(8,128)(2,1)}), bf16[4096,1024]{1,0:T(8,128)(2,1)}) %all-gather.33.cloned.1.call-update) | async-done | bytes 8388624 | tf_op jit(solution)/shard_map/all_gather | solution.py:80
  516.5 6.5 fusion.120
  525.4 11.2 fusion.121
  536.6 6.9 multiply_reduce_fusion.1
  548.8 110.1 %while.40 = (s32[]{:T(128)}, f32[16,1,256,64]{2,3,1,0:T(8,128)S(1)}, f32[16,1,256]{2,1,0:T(1,128)S(1)}, bf16[16,1,256,64]{3,2,1,0:T(8,128)(2,1)}, bf16[16,1,4096...) while((s32[]{:T(128)}, ...), condition=%wide.region_14.15_spmd.clone, body=%wide.region_12.14_spmd.clone.sunk | while | flops 412106496 | bytes 24308852 | solution.py:169
  658.9 23.3 %all_gather.83 = f32[16,1,4096]{2,1,0:T(1,128)S(1)} all-gather(f32[16,1,256]{2,1,0:T(1,128)S(1)} %get-tuple-element.848), channel_id=1, replica_groups=mesh['ctx'=16,'fsdp'=2] {'ctx'}, dimensions={2}, use_global_device_ids=true | all-gather | bytes 278528 | tf_op jit(solution)/shard_map/all_gather | solution.py:179
  682.3 19.5 %all_gather.85 = f32[16,1,4096]{2,1,0:T(1,128)} all-gather(f32[16,1,256]{2,1,0:T(1,128)S(1)} %get-tuple-element.159), channel_id=1, replica_groups=mesh['ctx'=16,'fsdp'=2] {'ctx'}, dimensions={2}, use_global_device_ids=true | all-gather | bytes 278528 | tf_op jit(solution)/shard_map/all_gather | solution.py:180
  707.7 191.3 %while.41 = (s32[]{:T(128)}, bf16[16,1,256,64]{2,3,1,0:T(8,128)(2,1)S(1)}, f32[16,1,256,64]{2,3,1,0:T(8,128)}, bf16[16,1,4096,64]{2,3,0,1:T(8,128)(2,1)}, bf16[1...) while((s32[]{:T(128)}, ...), condition=%wide.region_16.17_spmd.clone, body=%wide.region_15.16_spmd.clone.sunk | while | flops 545275904 | bytes 14996601 | solution.py:207
  712.4 3.9 fusion.182
  724.3 4.0 fusion.182
  736.3 3.9 fusion.182
  748.2 4.1 fusion.182
  760.4 3.9 fusion.182
  784.5 3.9 fusion.182
  796.4 3.9 fusion.182
  820.2 3.9 fusion.182
  844.0 3.9 fusion.182
  855.9 3.9 fusion.182
  867.8 3.9 fusion.182
  891.6 3.9 fusion.182
  906.6 10.7 fusion.109
  917.7 10.0 fusion.96
  927.8 28.2 %reduce-scatter.11.cloned.1.call-done = f32[512,1024]{0,1:T(8,128)} async-done(((f32[1024,1024]{0,1:T(8,128)}), f32[512,1024]{0,1:T(8,128)}) %reduce-scatter.11.cloned.1.call-update) | async-done | bytes 2097168 | tf_op jit(solution)/shard_map/reduce_scatter | solution.py:232
  956.1 57.1 %reduce-scatter.9.cloned.1.call-done = f32[512,1024]{0,1:T(8,128)} async-done(((f32[1024,1024]{0,1:T(8,128)}), f32[512,1024]{0,1:T(8,128)}) %reduce-scatter.9.cloned.1.call-update) | async-done | bytes 2097168 | tf_op jit(solution)/shard_map/reduce_scatter | solution.py:231
  1013.2 191.4 %reduce-scatter.17.cloned.1.call-done = f32[2048,1024]{1,0:T(8,128)} async-done(((f32[4096,1024]{1,0:T(8,128)}), f32[2048,1024]{1,0:T(8,128)}) %reduce-scatter.17.cloned.1.call-update) | async-done | bytes 8388624 | tf_op jit(solution)/shard_map/reduce_scatter | solution.py:241
  1204.6 191.4 %reduce-scatter.15.cloned.1.call-done = f32[512,4096]{1,0:T(8,128)} async-done(((f32[1024,4096]{1,0:T(8,128)}), f32[512,4096]{1,0:T(8,128)}) %reduce-scatter.15.cloned.1.call-update) | async-done | bytes 8388624 | tf_op jit(solution)/shard_map/reduce_scatter | solution.py:239
  1406.4 7.5 all-reduce.11
  1414.5 63.4 %all-reduce.9 = (f32[512]{0:T(512)}, f32[512]{0:T(512)}, f32[512]{0:T(512)}, f32[512]{0:T(512)}, f32[512]{0:T(512)}, /*index=5*/f32[2048]{0:T(1024)}, f32[512]{0:T(512)}, f32[512]{0:T(512)}, f32[512]{0:T(512)}) all-reduce(f32[512]{0:T(512)S(1)} %dynamic-slice.1, ...), channel_id=1, replica_groups=mesh['ctx'=16,'fsdp'=2] {'ctx'}, use_global_device_ids=true, to_apply=%region_27.28 | all-reduce | flops 6144 | bytes 49152 | tf_op jit(solution)/shard_map/psum | solution.py:246
  1483.8 355.3 %all-reduce.14.cloned.1.call-done = (f32[512,1024]{0,1:T(8,128)}, f32[512,1024]{0,1:T(8,128)}, f32[512,1024]{0,1:T(8,128)}, f32[512,1024]{1,0:T(8,128)}, f32[512,4096]{1,0:T(8,128)}, /*index=5*/f32[2048,1024]{1,0:T(8,128)}) async-done(((f32[512,1024]{0,1:T(8,128)}, f32[512,1024]{0,1:T(8,128)}, f32[512,1024]{0,1:T(8,128)}, f32[512,1024]{1,0:T(8,128)}, f32[512,4096]{1,0:T(8,128)}, ...) | async-done | bytes 25165840 | tf_op jit(solution)/shard_map/psum | solution.py:246
  1849.2 8.5 copy.125
  (392 shorter events, 406.0 us)
Async XLA Ops:
  7.2 72.9 %copy-start.6 = (bf16[1,256,1024]{2,1,0:T(8,128)(2,1)S(1)}, bf16[1,256,1024]{2,1,0:T(8,128)(2,1)}, u32[]{:S(2)}) copy-start(bf16[1,256,1024]{2,1,0:T(8,128)(2,1)} %param.24) | copy-start | bytes 1572868
  7.2 38.2 %all-gather.25.cloned.1.call-start = ((), (), s32[]{:S(2)}) async-start(), calls=%async_computation.9 | async-start | bytes 3145728 | tf_op jit(solution)/shard_map/all_gather | solution.py:69
  7.9 72.1 %all-gather.21.cloned.1.call-start = ((), (), s32[]{:S(2)}) async-start(), calls=%async_computation.7 | async-start | bytes 3145728 | tf_op jit(solution)/shard_map/all_gather | solution.py:68
  8.7 113.0 %all-gather.19.cloned.1.call-start = ((), (), s32[]{:S(2)}) async-start(), calls=%async_computation.6 | async-start | bytes 3145728 | tf_op jit(solution)/shard_map/all_gather | solution.py:67
  9.4 185.4 %all-gather.27.cloned.1.call-start = ((), (), s32[]{:S(2)}) async-start(), calls=%async_computation.10 | async-start | bytes 8912896 | tf_op jit(solution)/shard_map/all_gather | solution.py:94
  48.9 223.8 %all-gather.23.cloned.1.call-start = ((), (), s32[]{:S(2)}) async-start(), calls=%async_computation.8 | async-start | bytes 8912896 | tf_op jit(solution)/shard_map/all_gather | solution.py:93
  83.4 287.9 %all-gather.29.cloned.1.call-start = ((), (), s32[]{:S(2)}) async-start(), calls=%async_computation.11 | async-start | bytes 3145728 | tf_op jit(solution)/shard_map/all_gather | solution.py:70
  84.0 1.7 copy-start.20
  84.0 6.1 copy-start.21
  84.0 10.7 copy-start.22
  84.0 15.2 copy-start.23
  84.0 19.7 %copy-start.19 = (bf16[2048]{0:T(1024)(128)(2,1)S(1)}, bf16[2048]{0:T(1024)(128)(2,1)}, u32[]{:S(2)}) copy-start(bf16[2048]{0:T(1024)(128)(2,1)} %param.36) | copy-start | bytes 12292
  84.1 24.3 %copy-start.24 = (bf16[512]{0:T(512)(128)(2,1)S(1)}, bf16[512]{0:T(512)(128)(2,1)}, u32[]{:S(2)}) copy-start(bf16[512]{0:T(512)(128)(2,1)} %param.38) | copy-start | bytes 3076
  84.1 28.8 %copy-start.25 = (bf16[512]{0:T(512)(128)(2,1)S(1)}, bf16[512]{0:T(512)(128)(2,1)}, u32[]{:S(2)}) copy-start(bf16[512]{0:T(512)(128)(2,1)} %param.39) | copy-start | bytes 3076
  84.1 33.2 %copy-start.26 = (bf16[512]{0:T(512)(128)(2,1)S(1)}, bf16[512]{0:T(512)(128)(2,1)}, u32[]{:S(2)}) copy-start(bf16[512]{0:T(512)(128)(2,1)} %param.40) | copy-start | bytes 3076
  84.1 37.6 %copy-start.18 = (s32[1,4096]{1,0:T(1,128)S(1)}, s32[1,4096]{1,0:T(1,128)}, u32[]{:S(2)}) copy-start(s32[1,4096]{1,0:T(1,128)} %param.25) | copy-start | bytes 49156
  84.1 326.8 %all-gather.31.cloned.1.call-start = ((), (), s32[]{:S(2)}) async-start(), calls=%async_computation.12 | async-start | bytes 12582912 | tf_op jit(solution)/shard_map/all_gather | solution.py:78
  84.9 431.6 %all-gather.33.cloned.1.call-start = ((), (), s32[]{:S(2)}) async-start(), calls=%async_computation.13 | async-start | bytes 12582912 | tf_op jit(solution)/shard_map/all_gather | solution.py:80
  85.6 621.0 %all-gather.35.cloned.1.call-start = ((), (), s32[]{:S(2)}) async-start(), calls=%async_computation.14 | async-start | bytes 8912896 | tf_op jit(solution)/shard_map/all_gather | solution.py:175
  90.1 120.4 %copy-start = (bf16[16,1,256,64]{2,3,1,0:T(8,128)(2,1)}, bf16[16,1,256,64]{2,3,1,0:T(8,128)(2,1)S(1)}, u32[]{:S(2)}) copy-start(bf16[16,1,256,64]{2,3,1,0:T(8,128)(2,1)S(1)} %fusion.118) | copy-start | bytes 1572868
  124.3 0.8 copy-start.12
  125.1 581.5 %all-gather.37.cloned.1.call-start = ((), (), s32[]{:S(2)}) async-start(), calls=%async_computation.15 | async-start | bytes 8912896 | tf_op jit(solution)/shard_map/all_gather | solution.py:176
  272.7 15.8 copy-start.2
  371.3 1.0 copy-start.17
  516.5 6.8 copy-start.13
  523.0 2.3 copy-start.28
  525.0 11.6 copy-start.5
  536.6 6.9 copy-start.16
  536.6 7.3 copy-start.14
  545.7 382.0 %reduce-scatter.13.cloned.1.call-start = ((), (), s32[]{:S(2)}) async-start(), calls=%async_computation.19 | async-start | bytes 6291456 | tf_op jit(solution)/shard_map/reduce_scatter | solution.py:233
  548.7 379.2 %reduce-scatter.7.cloned.1.call-start = ((), (), s32[]{:S(2)}) async-start(), calls=%async_computation.16 | async-start | bytes 6291456 | tf_op jit(solution)/shard_map/reduce_scatter | solution.py:230
  658.9 43.0 %copy-start.4 = (f32[16,1,256,64]{2,3,1,0:T(8,128)}, f32[16,1,256,64]{2,3,1,0:T(8,128)S(1)}, u32[]{:S(2)}) copy-start(f32[16,1,256,64]{2,3,1,0:T(8,128)S(1)} %get-tuple-element.158) | copy-start | bytes 3145732
  701.9 0.8 copy-start.8
  706.5 1.2 copy-start.1
  706.5 249.5 %reduce-scatter.11.cloned.1.call-start = ((), (), s32[]{:S(2)}) async-start(), calls=%async_computation.18 | async-start | bytes 6291456 | tf_op jit(solution)/shard_map/reduce_scatter | solution.py:232
  707.7 193.4 %copy-start.7 = (bf16[1,256,1024]{2,1,0:T(8,128)(2,1)S(1)}, bf16[1,256,1024]{2,1,0:T(8,128)(2,1)}, u32[]{:S(2)}) copy-start(bf16[1,256,1024]{2,1,0:T(8,128)(2,1)} %param.24) | copy-start | bytes 1572868
  900.3 0.8 copy-start.10
  903.8 109.4 %reduce-scatter.9.cloned.1.call-start = ((), (), s32[]{:S(2)}) async-start(), calls=%async_computation.17 | async-start | bytes 6291456 | tf_op jit(solution)/shard_map/reduce_scatter | solution.py:231
  906.6 298.0 %reduce-scatter.17.cloned.1.call-start = ((), (), s32[]{:S(2)}) async-start(), calls=%async_computation.21 | async-start | bytes 25165824 | tf_op jit(solution)/shard_map/reduce_scatter | solution.py:241
  917.4 478.5 %reduce-scatter.15.cloned.1.call-start = ((), (), s32[]{:S(2)}) async-start(), calls=%async_computation.20 | async-start | bytes 25165824 | tf_op jit(solution)/shard_map/reduce_scatter | solution.py:239
  927.7 911.4 %all-reduce.14.cloned.1.call-start = ((), (), s32[]{:S(2)}) async-start(), calls=%async_computation.22 | async-start | bytes 50331648 | tf_op jit(solution)/shard_map/psum | solution.py:246
  1396.0 0.7 copy-start.27
  1396.0 6.8 copy-start.9
  1398.5 7.6 copy-start.3
  1406.1 74.4 %copy-start.11 = (bf16[1,256,16,64]{1,3,0,2:T(8,128)(2,1)S(1)}, bf16[1,256,16,64]{1,3,0,2:T(8,128)(2,1)}, u32[]{:S(2)}) copy-start(bf16[1,256,16,64]{1,3,0,2:T(8,128)(2,1)} %copy-done.10) | copy-start | bytes 1572868
  1842.0 5.9 copy-start.15
  1847.9 9.8 slice-start
  1849.2 8.5 slice-start.1
Sparse Core Ops, SparseCore 0:
  9.6 35.8 all-gather.24
  46.9 33.0 all-gather.20
  81.6 33.3 all-gather.18
  117.0 77.7 all-gather.26
  196.8 75.8 all-gather.22
  274.1 31.2 all-gather.28
  306.9 103.9 all-gather.30
  412.5 103.9 all-gather.32
  518.7 77.7 all-gather.34
  599.0 76.7 all-gather.36
  678.1 52.8 reduce-scatter.12
  733.7 54.3 reduce-scatter.6
  903.9 52.0 reduce-scatter.10
  958.8 54.3 reduce-scatter.8
  1015.3 189.1 reduce-scatter.16
  1206.7 189.1 reduce-scatter.14
  1401.3 437.7 all-reduce.13
where the time goes:
time: 1880 us; the launch traced here: 1870 us
  waiting for transfers between devices  1150 us (61%)
  matrix products  452 us (24%)
  blocking collectives  155 us (8%)
  local copies, waits for them, and re-layouts  76.5 us (4%)
  other arithmetic  20 us (1%)
    psum x1, waiting for transfers between devices, body(): lax.psum((shards[0], shards[1], shards[2], shards[3], shards[4], shards[5...  355 us
    reduce_scatter x1, waiting for transfers between devices, body(): lax.psum_scatter(grad_w_up, 'fsdp', scatter_dimension=0, tiled=True)  191 us
    reduce_scatter x1, waiting for transfers between devices, body(): lax.psum_scatter(grad_w_down, 'fsdp', scatter_dimension=0, tiled=True)  191 us
    all_gather x1, waiting for transfers between devices, body(): lax.all_gather(w_down, 'fsdp', axis=0, tiled=True)  89.4 us
    dot_general x32, matrix products, scores_of(): jnp.einsum('sre,sle->srl', query_part, key_part, preferred_element_type=j...  77.7 us
    all_gather x1, waiting for transfers between devices, body(): lax.all_gather(value_local, 'ctx', axis=2, tiled=True)  69.1 us
    psum x1, blocking collectives, body(): lax.psum((shards[0], shards[1], shards[2], shards[3], shards[4], shards[5...  63.4 us
    dot_general x16, matrix products, owner_head(): jnp.einsum('srl,sre->sle', d_scores, query_part, preferred_element_type=j...  62.4 us
  transfers between devices with their start and end apart: 17, of which 11 were waited for; matrix products, arithmetic and copies ran while one was open for 28% of the time, Pallas kernels for 0%

commit v1 on v0

v1 whole, which is shorter than its diff:
```python
import functools
import math

import jax
import jax.numpy as jnp
from jax import lax
from jax.experimental import pallas as pl
from jax.experimental.pallas import tpu as pltpu
from jax.sharding import PartitionSpec as P

HEADS = 16
LOG2E = 1.4426950408889634
NEG = -1e30
BF = jnp.bfloat16
F32 = jnp.float32


def layer_norm(hidden, gain, shift):
    mean = jnp.mean(hidden, axis=-1, keepdims=True)
    centred = hidden - mean
    variance = jnp.mean(centred * centred, axis=-1, keepdims=True)
    return centred * lax.rsqrt(variance + 1e-05) * gain + shift


def gelu_exact(value):
    return jax.nn.gelu(value, approximate=False)


def dot(left, right, on_left, on_right):
    return lax.dot_general(
        left, right, (((on_left,), (on_right,)), ((), ())), preferred_element_type=F32
    )


def flip(value, axis, bit, size):
    return lax.ppermute(value, axis, [(i, i ^ bit) for i in range(size)])


def forward_kernel(
    lo_ref, hi_ref, in_lo_ref, in_hi_ref, q_ref, k_ref, vt_ref, start_ref, end_ref,
    out_ref, lse_ref, total_ref, *, bk, scale
):
    i = pl.program_id(0)
    bq = q_ref.shape[0]
    q = q_ref[...]
    start, end = start_ref[...], end_ref[...]
    total_ref[...] = jnp.zeros_like(total_ref)

    def step(j, carry, masked):
        peak, norm = carry
        at = pl.multiple_of(j * bk, bk)
        s = dot(k_ref[pl.ds(at, bk), :], q, 1, 1) * (scale * LOG2E)
        if masked:
            at_key = lax.broadcasted_iota(jnp.int32, (bk, bq), 0) + at
            s = jnp.where((at_key >= start) & (at_key < end), s, NEG)
        new_peak = jnp.maximum(peak, jnp.max(s, axis=0, keepdims=True))
        p = jnp.exp2(s - new_peak)
        shrink = jnp.exp2(peak - new_peak)
        norm = norm * shrink + jnp.sum(p, axis=0, keepdims=True)
        total_ref[...] = total_ref[...] * shrink + dot(vt_ref[:, pl.ds(at, bk)], p.astype(BF), 1, 0)
        return new_peak, norm

    lo, hi, in_lo, in_hi = lo_ref[i], hi_ref[i], in_lo_ref[i], in_hi_ref[i]
    carry = (jnp.full((1, bq), NEG, F32), jnp.zeros((1, bq), F32))
    carry = lax.fori_loop(in_lo, in_hi, lambda j, c: step(j, c, False), carry)
    carry = lax.fori_loop(lo, in_lo, lambda j, c: step(j, c, True), carry)
    peak, norm = lax.fori_loop(in_hi, hi, lambda j, c: step(j, c, True), carry)
    out_ref[...] = total_ref[...] / norm
    lse_ref[...] = peak + jnp.log2(norm)


def block_ranges(starts, ends, rows, others):
    first, last = starts.reshape(-1, rows), ends.reshape(-1, rows)
    lo = first[:, 0] // others
    hi = (last[:, -1] + others - 1) // others
    in_lo = jnp.clip((first[:, -1] + others - 1) // others, lo, hi)
    in_hi = jnp.clip(last[:, 0] // others, in_lo, hi)
    return lo, hi, in_lo, in_hi


def attention_forward(q, k, vt, starts, ends, scale, bq=1024, bk=512):
    count, d = q.shape
    length = k.shape[0]
    bq = min(bq, count)
    ranges = block_ranges(starts, ends, bq, bk)
    row = lambda: pl.BlockSpec((1, bq), lambda i, *_: (0, i))
    whole = lambda shape: pl.BlockSpec(shape, lambda i, *_: (0, 0))
    return pl.pallas_call(
        functools.partial(forward_kernel, bk=bk, scale=scale),
        out_shape=(
            jax.ShapeDtypeStruct((d, count), F32),
            jax.ShapeDtypeStruct((1, count), F32),
        ),
        grid_spec=pltpu.PrefetchScalarGridSpec(
            num_scalar_prefetch=4,
            grid=(count // bq,),
            in_specs=[
                pl.BlockSpec((bq, d), lambda i, *_: (i, 0)),
                whole((length, d)),
                whole((d, length)),
                row(),
                row(),
            ],
            out_specs=[pl.BlockSpec((d, bq), lambda i, *_: (0, i)), row()],
            scratch_shapes=[pltpu.VMEM((d, bq), F32)],
        ),
        compiler_params=pltpu.CompilerParams(vmem_limit_bytes=40 << 20),
        cost_estimate=pl.CostEstimate(
            flops=4 * count * length * d, bytes_accessed=length * d * 16, transcendentals=count * length
        ),
        name="attention_forward",
    )(*ranges, q, k, vt, starts[None], ends[None])


def backward_kernel(
    lo_ref, hi_ref, in_lo_ref, in_hi_ref, k_ref, v_ref, kt_ref, q_ref, do_ref, lse_ref, delta_ref, start_ref,
    end_ref, dk_ref, dv_ref, dqt_ref, *, bq, scale
):
    j = pl.program_id(0)
    bk = k_ref.shape[0]

    @pl.when(j == 0)
    def _():
        dqt_ref[...] = jnp.zeros_like(dqt_ref)

    k, v, kt = k_ref[...], v_ref[...], kt_ref[...]
    dk_ref[...] = jnp.zeros_like(dk_ref)
    dv_ref[...] = jnp.zeros_like(dv_ref)

    def step(i, masked):
        at = pl.multiple_of(i * bq, bq)
        row = pl.ds(at, bq)
        q, do = q_ref[row, :], do_ref[row, :]
        s = dot(k, q, 1, 1) * (scale * LOG2E) - lse_ref[:, row]
        if masked:
            at_key = lax.broadcasted_iota(jnp.int32, (bk, bq), 0) + j * bk
            s = jnp.where((at_key >= start_ref[:, row]) & (at_key < end_ref[:, row]), s, NEG)
        p = jnp.exp2(s)
        dp = dot(v, do, 1, 1)
        dv_ref[...] += dot(p.astype(BF), do, 1, 0)
        ds = (p * (dp - delta_ref[:, row])).astype(BF)
        dk_ref[...] += dot(ds, q, 1, 0)
        dqt_ref[:, row] += dot(kt, ds, 1, 0)

    lo, hi, in_lo, in_hi = lo_ref[j], hi_ref[j], in_lo_ref[j], in_hi_ref[j]
    pl.loop(in_lo, in_hi)(lambda i: step(i, False))
    pl.loop(lo, in_lo)(lambda i: step(i, True))
    pl.loop(in_hi, hi)(lambda i: step(i, True))


def attention_backward(q, k, v, kt, do, lse, delta, starts, ends, ranges, scale, bq, bk):
    count, d = q.shape
    length = k.shape[0]
    whole = lambda shape: pl.BlockSpec(shape, lambda j, *_: (0, 0))
    keys = lambda: pl.BlockSpec((bk, d), lambda j, *_: (j, 0))
    return pl.pallas_call(
        functools.partial(backward_kernel, bq=bq, scale=scale),
        out_shape=(
            jax.ShapeDtypeStruct((length, d), F32),
            jax.ShapeDtypeStruct((length, d), F32),
            jax.ShapeDtypeStruct((d, count), F32),
        ),
        grid_spec=pltpu.PrefetchScalarGridSpec(
            num_scalar_prefetch=4,
            grid=(length // bk,),
            in_specs=[
                keys(),
                keys(),
                pl.BlockSpec((d, bk), lambda j, *_: (0, j)),
                whole((count, d)),
                whole((count, d)),
                whole((1, count)),
                whole((1, count)),
                whole((1, count)),
                whole((1, count)),
            ],
            out_specs=[keys(), keys(), whole((d, count))],
        ),
        compiler_params=pltpu.CompilerParams(vmem_limit_bytes=48 << 20),
        cost_estimate=pl.CostEstimate(
            flops=10 * count * length * d, bytes_accessed=length * d * 40, transcendentals=count * length
        ),
        name="attention_backward",
    )(*ranges, k, v, kt, q, do, lse, delta, starts[None], ends[None])


def body(ctx, fsdp, tokens, segments, w_query, w_key, w_value, w_out, b_query, b_value, b_out, gain_one, shift_one,
         w_up, b_up, w_down, b_down, gain_two, shift_two, cotangent):
    _, block, width = tokens.shape
    heads = HEADS
    d = width // heads
    scale = 1.0 / math.sqrt(d)
    parts = ctx // heads
    mine = block // parts
    length = ctx * block
    count = length // parts
    hidden = w_up.shape[1]
    shard = w_query.shape[0]
    me = lax.axis_index("ctx")
    row = lax.axis_index("fsdp")
    head, part = me // parts, me % parts
    core = me % 2
    cut = lambda a, at, size, axis: lax.dynamic_slice_in_dim(a, at, size, axis)

    def gather_small(a):
        if fsdp == 2:
            other = flip(a, "fsdp", 1, 2)
            return jnp.concatenate([jnp.where(row == 0, a, other), jnp.where(row == 0, other, a)], axis=0)
        return lax.all_gather(a, "fsdp", axis=0, tiled=True)

    def gather_weight(w):
        if fsdp != 2:
            return lax.all_gather(w, "fsdp", axis=0, tiled=True)
        rows = w.shape[0]
        half = rows // 2
        near = flip(cut(w, core * half, half, 0), "fsdp", 1, 2)
        far = flip(near, "ctx", 1, ctx)
        whole = jnp.zeros((2 * rows, w.shape[1]), w.dtype)
        whole = lax.dynamic_update_slice_in_dim(whole, w, row * rows, 0)
        whole = lax.dynamic_update_slice_in_dim(whole, near, (1 - row) * rows + core * half, 0)
        return lax.dynamic_update_slice_in_dim(whole, far, (1 - row) * rows + (1 - core) * half, 0)

    everyone = lax.all_gather(tokens[0], "ctx", axis=0, tiled=True)
    slices = jnp.concatenate([cut(w, head * d, d, 1) for w in (w_query, w_key, w_value)], axis=1)
    w_head = gather_small(slices)
    small = jnp.stack([b_query, b_value, b_out, gain_one, shift_one, b_down, gain_two, shift_two])
    small = jnp.concatenate([small.reshape(-1), b_up])[None]
    small = gather_small(small) if fsdp == 2 else lax.all_gather(small, "fsdp", axis=0, tiled=True)
    eight = small[:, : 8 * shard].reshape(-1, 8, shard).transpose(1, 0, 2).reshape(8, width).astype(F32)
    bq_, bv_, bo, gain1, shift1, bd, gain2, shift2 = (eight[i] for i in range(8))
    bu = small[:, 8 * shard :].reshape(hidden).astype(F32)
    wo = gather_weight(w_out)
    wu = gather_weight(w_up)
    wd = gather_weight(w_down)
    wq, wk, wv = gather_weight(w_query), gather_weight(w_key), gather_weight(w_value)

    projected = dot(everyone, w_head, 1, 0)
    my_bias = jnp.concatenate([cut(bq_, head * d, d, 0), jnp.zeros((d,), F32), cut(bv_, head * d, d, 0)])
    projected = (projected + my_bias).astype(BF)
    own_part = lambda a: cut(a.reshape((ctx, block) + a.shape[1:]), part * mine, mine, 1).reshape(
        (count,) + a.shape[1:]
    )
    q = own_part(projected[:, :d])
    k, v = projected[:, d : 2 * d], projected[:, 2 * d :]
    kt, vt = k.T, v.T
    seg = segments[0]
    all_numbers = seg[None, :]
    starts_all = jnp.sum(all_numbers < seg[:, None], axis=1, dtype=jnp.int32)
    ends_all = jnp.sum(all_numbers <= seg[:, None], axis=1, dtype=jnp.int32)
    starts, ends = own_part(starts_all), own_part(ends_all)

    attended_t, lse = attention_forward(q, k, vt, starts, ends, scale)
    outgoing = attended_t.astype(BF).reshape(d, ctx, mine).transpose(1, 0, 2)
    incoming = lax.all_to_all(outgoing, "ctx", 0, 0, tiled=True)
    attended = incoming.reshape(heads, parts, d, mine).transpose(1, 3, 0, 2).reshape(block, width)

    inputs = tokens[0]
    branch = dot(attended, wo, 1, 0) + bo
    first, first_pull = jax.vjp(layer_norm, inputs.astype(F32) + branch, gain1, shift1)
    first_low = first.astype(BF)
    hidden_pre = dot(first_low, wu, 1, 0) + bu
    active, active_pull = jax.vjp(gelu_exact, hidden_pre)
    active_low = active.astype(BF)
    second = dot(active_low, wd, 1, 0) + bd
    output, out_pull = jax.vjp(layer_norm, first + second, gain2, shift2)
    d_second, grad_gain_two, grad_shift_two = out_pull(cotangent[0].astype(F32))
    d_second_low = d_second.astype(BF)
    (d_hidden,) = active_pull(dot(d_second_low, wd, 1, 1))
    d_hidden_low = d_hidden.astype(BF)
    d_first = d_second + dot(d_hidden_low, wu, 1, 1)
    d_branch, grad_gain_one, grad_shift_one = first_pull(d_first)
    d_branch_low = d_branch.astype(BF)
    d_attended_t = dot(wo, d_branch_low, 1, 1).astype(BF)
    outgoing = d_attended_t.reshape(heads, d, parts, mine).transpose(0, 2, 1, 3).reshape(ctx, d, mine)
    do_t = lax.all_to_all(outgoing, "ctx", 0, 0, tiled=True)
    do = do_t.transpose(0, 2, 1).reshape(count, d)
    delta = jnp.sum(
        attended_t.reshape(d, ctx, mine) * do_t.transpose(1, 0, 2).astype(F32), axis=0
    ).reshape(1, count)

    bits = lambda n: [1 << i for i in range(n.bit_length() - 1)]

    def reduce_matrix(left, right, first_bits):
        rows, columns = left.shape[1], right.shape[1]
        order = first_bits + [(a, b) for a, n in (("fsdp", fsdp), ("ctx", ctx)) for b in bits(n) if (a, b) not in first_bits]
        place = [("fsdp", b) for b in reversed(bits(fsdp))] + [("ctx", b) for b in bits(ctx)]
        shape = [2] * len(place)
        chosen = lambda a, b: (lax.axis_index(a) // b) % 2
        size = {"fsdp": fsdp, "ctx": ctx}
        axis, bit = order[0]
        at = place.index((axis, bit))
        halves = left.reshape([left.shape[0]] + shape + [-1])
        pick = lambda which: lax.dynamic_index_in_dim(halves, which, at + 1, keepdims=False).reshape(left.shape[0], -1)
        own = chosen(axis, bit)
        sent = dot(pick(1 - own), right, 0, 0).astype(BF)
        total = (dot(pick(own), right, 0, 0) + flip(sent, axis, bit, size[axis]).astype(F32)).astype(BF)
        place.remove((axis, bit))
        total = total.reshape([2] * len(place) + [-1, columns])
        for axis, bit in order[1:]:
            at = place.index((axis, bit))
            own = chosen(axis, bit)
            keep = lax.dynamic_index_in_dim(total, own, at, keepdims=False)
            send = lax.dynamic_index_in_dim(total, 1 - own, at, keepdims=False)
            total = (keep.astype(F32) + flip(send, axis, bit, size[axis]).astype(F32)).astype(BF)
            place.remove((axis, bit))
        return total

    def spread_matrix(total, rows, columns):
        every = lax.all_gather(total, "ctx", axis=0, tiled=False)
        n = len(bits(ctx))
        every = every.reshape([2] * n + [-1, columns])
        every = every.transpose(list(reversed(range(n))) + [n, n + 1])
        return every.reshape(rows, columns).astype(F32)

    down_bits = [("ctx", 1), ("fsdp", 1), ("ctx", 2)]
    up_bits = [("ctx", 1), ("ctx", 2), ("fsdp", 1)]
    grad_w_down = spread_matrix(reduce_matrix(active_low, d_second_low, down_bits), w_down.shape[0], width)
    grad_w_up = spread_matrix(reduce_matrix(first_low, d_hidden_low, up_bits), shard, hidden)
    grad_w_out = spread_matrix(reduce_matrix(attended, d_branch_low, down_bits), shard, width)

    vectors = [
        jnp.sum(d_branch, axis=0), grad_gain_one, grad_shift_one, jnp.sum(d_second, axis=0), grad_gain_two,
        grad_shift_two,
    ]
    vectors = jnp.concatenate(
        [jnp.stack(vectors).reshape(6, fsdp, shard).transpose(1, 0, 2).reshape(fsdp, -1),
         jnp.sum(d_hidden, axis=0).reshape(fsdp, -1)], axis=1,
    )
    for bit in reversed(bits(fsdp)):
        own = (row // bit) % 2
        pair = vectors.reshape(2, -1, vectors.shape[1])
        keep = lax.dynamic_index_in_dim(pair, own, 0, keepdims=False)
        send = lax.dynamic_index_in_dim(pair, 1 - own, 0, keepdims=False)
        vectors = keep + flip(send, "fsdp", bit, fsdp)
    for bit in bits(ctx):
        vectors = vectors + flip(vectors, "ctx", bit, ctx)
    six = vectors[0, : 6 * shard].reshape(6, shard)
    grad_b_up = vectors[0, 6 * shard :]

    bq, bk = min(512, count), 512
    ranges = block_ranges(starts_all, ends_all, bk, bq * parts)
    dk, dv, dqt = attention_backward(q, k, v, kt, do, lse, delta, starts, ends, ranges, scale, bq, bk)
    dq = (dqt.T * scale).astype(BF)
    dk, dv = (dk * scale).astype(BF), dv.astype(BF)
    share = lambda a: a.reshape(ctx, -1, d)
    if parts == 1:
        outgoing = jnp.concatenate([dq, dk, dv], axis=1).reshape(ctx, block, 3 * d)
        incoming = lax.all_to_all(outgoing, "ctx", 0, 0, tiled=True)
        grads = [incoming[:, :, i * d : (i + 1) * d].transpose(1, 0, 2).reshape(block, width) for i in range(3)]
        everyone_q = everyone
    else:
        back = lambda a: lax.all_to_all(share(a), "ctx", 0, 0, tiled=True).reshape(heads, parts, -1, d)
        dq_in = back(dq).transpose(1, 2, 0, 3).reshape(block, width)
        summed = lambda a: jnp.sum(back(a).astype(F32), axis=1).astype(BF).transpose(1, 0, 2).reshape(block, width)
        grads = [dq_in, summed(dk), summed(dv)]
        everyone_q = own_part(everyone)
    token_grad = d_branch + dot(grads[0], wq, 1, 1) + dot(grads[1], wk, 1, 1) + dot(grads[2], wv, 1, 1)

    sums = jnp.concatenate(
        [jnp.sum(dq.astype(F32), axis=0), jnp.zeros((d,), F32), jnp.sum(dv.astype(F32), axis=0)]
    )
    grad_head = jnp.concatenate([dot(everyone_q, dq, 0, 0), dot(everyone, dk, 0, 0), dot(everyone, dv, 0, 0)], axis=1)
    grad_head = lax.psum_scatter(grad_head.astype(BF), "fsdp", scatter_dimension=0, tiled=True) if fsdp != 2 else (
        cut(grad_head, row * shard, shard, 0)
        + flip(cut(grad_head, (1 - row) * shard, shard, 0).astype(BF), "fsdp", 1, 2).astype(F32)
    ).astype(BF)
    sums = jnp.broadcast_to(lax.psum(sums, "fsdp")[None], (16, 3 * d)).astype(BF)
    every = lax.all_gather(jnp.concatenate([grad_head, sums]), "ctx", axis=0, tiled=False)
    every = every.astype(F32).reshape(heads, parts, shard + 16, 3, d).sum(axis=1)
    every = every.transpose(2, 1, 0, 3).reshape(3, shard + 16, width)
    bias_q = cut(every[0, shard], row * shard, shard, 0)
    bias_v = cut(every[2, shard], row * shard, shard, 0)

    return (
        output[None].astype(BF),
        token_grad[None].astype(BF),
        every[0, :shard],
        every[1, :shard],
        every[2, :shard],
        grad_w_out,
        bias_q,
        bias_v,
        six[0],
        six[1],
        six[2],
        grad_w_up,
        grad_b_up,
        grad_w_down,
        six[3],
        six[4],
        six[5],
    )


def solution(mesh):
    line, matrix, rows = P("fsdp"), P("fsdp", None), P("fsdp", "ctx", None)
    placed = (
        (rows, matrix) + (matrix,) * 4 + (line,) * 5 + (matrix, line, matrix) + (line,) * 3 + (rows,)
    )
    outs = (rows, rows) + (matrix,) * 4 + (line,) * 5 + (matrix, line, matrix) + (line,) * 3
    return jax.shard_map(
        functools.partial(body, mesh.shape["ctx"], mesh.shape["fsdp"]),
        mesh=mesh,
        in_specs=placed,
        out_specs=outs,
        check_vma=False,
    )
```

time: 1880 us -> 701 us (0.37)
  waiting for transfers between devices: 1150 us -> 290 us
  matrix products: 452 us -> 76.4 us
  blocking collectives: 155 us -> 4.92 us
  Pallas kernels: 0 us -> 79.3 us
  local copies, waits for them, and re-layouts: 76.5 us -> 142 us
  starting transfers between devices: 1.46 us -> 44.1 us
    reduce_scatter x6 -> x0, waiting for transfers between devices: 468 us -> none  [the longest x1 191 us: body(): lax.psum_scatter(grad_w_up, 'fsdp', scatter_dimension=0, tiled=True)]
    dot_general x146 -> x19, matrix products: 452 us -> 76.4 us  [dot(): lax.dot_general(left, right, (((on_left,), (on_right,)), ((), ())), prefe...]
    psum x1 -> x0, waiting for transfers between devices: 355 us -> none  [body(): lax.psum((shards[0], shards[1], shards[2], shards[3], shards[4], shards[5...]
    all_gather x10 -> x5, waiting for transfers between devices: 318 us -> 0.01 us  [the longest x3 0.01 us: spread_matrix(): every = lax.all_gather(total, 'ctx', axis=0, tiled=False)]
    ppermute x0 -> x35, waiting for transfers between devices: none -> 284 us  [flip(): return lax.ppermute(value, axis, [(i, i ^ bit) for i in range(size)])]
    all_gather x11 -> x0, blocking collectives: 83.9 us -> none  [the longest x1 23.3 us: body(): lax.all_gather(log_total, 'ctx', axis=2, tiled=True)]
    pallas_call x0 -> x2, Pallas kernels: none -> 79.3 us  [the longest x1 47.6 us: attention_backward(): pl.pallas_call(functools.partial(backward_kernel, bq=bq, scale=scale), ou...]
    psum x1, blocking collectives: 63.4 us -> 4.92 us  [body(): lax.psum(sums, 'fsdp')[None]]
  transfers between devices with their start and end apart: 17 -> 43, of which waited for: 11 -> 21; matrix products, arithmetic and copies ran while one was open for 28% -> 28% of each run, Pallas kernels for 0% -> 11%
where the time goes in v1:
time: 701 us; the launch traced here: 691 us
  waiting for transfers between devices  290 us (41%)
  local copies, waits for them, and re-layouts  142 us (20%)
  Pallas kernels  79.3 us (11%)
  matrix products  76.4 us (11%)
  starting transfers between devices  44.1 us (6%)
  other arithmetic  38.7 us (6%)
  between operations  15.6 us (2%)
    ppermute x35, waiting for transfers between devices, flip(): return lax.ppermute(value, axis, [(i, i ^ bit) for i in range(size)])  284 us
    dot_general x19, matrix products, dot(): lax.dot_general(left, right, (((on_left,), (on_right,)), ((), ())), prefe...  76.4 us
    pallas_call x1, Pallas kernels, attention_backward(): pl.pallas_call(functools.partial(backward_kernel, bq=bq, scale=scale), ou...  47.6 us
    pallas_call x1, Pallas kernels, attention_forward(): pl.pallas_call(functools.partial(forward_kernel, bk=bk, scale=scale), out...  31.7 us
    ppermute x35, starting transfers between devices, flip(): return lax.ppermute(value, axis, [(i, i ^ bit) for i in range(size)])  28.8 us
    unnamed x106, local copies, waits for them, and re-layouts  24.9 us
    dynamic_slice x12, local copies, waits for them, and re-layouts, body(): cut = lambda a, at, size, axis: lax.dynamic_slice_in_dim(a, at, size, axis)  16.8 us
    convert_element_type x3, local copies, waits for them, and re-layouts, spread_matrix(): return every.reshape(rows, columns).astype(F32)  16.1 us
  transfers between devices with their start and end apart: 43, of which 21 were waited for; matrix products, arithmetic and copies ran while one was open for 28% of the time, Pallas kernels for 11%

profile of v1, /device:TPU:0, one launch (start us, length us, event | category | flops | bytes accessed | tf_op | source)
XLA Modules:
  0.0 690.7 jit_solution(7280394351151081019)
XLA Ops:
  14.1 3.0 collective-permute-start.1
  24.4 3.2 constant_dynamic-slice_fusion.9
  31.1 15.4 %convert_reduce_fusion = (s32[4096]{0:T(1024)S(1)}, s32[4096]{0:T(1024)S(1)}) fusion(s32[4096]{0:T(1024)S(1)} %bitcast.350), kind=kLoop, calls=%fused_computation | loop fusion | flops 100655104 | bytes 49152 | tf_op jit(solution)/shard_map/reduce_sum | solution.py:249
  49.7 4.8 broadcast_in_dim.17
  61.9 24.0 %collective-permute-done.6 = bf16[1024,1024]{1,0:T(8,128)(2,1)} collective-permute-done((bf16[1024,1024]{1,0:T(8,128)(2,1)}, bf16[1024,1024]{1,0:T(8,128)(2,1)}, u32[]{:S(2)}, u32[]{:S(2)}) %collective-permute-start.6) | collective-permute-done | bytes 2097184 | tf_op jit(solution)/shard_map/ppermute | solution.py:36
  85.9 43.5 %collective-permute-done.4 = bf16[256,4096]{1,0:T(8,128)(2,1)} collective-permute-done((bf16[256,4096]{1,0:T(8,128)(2,1)}, bf16[256,4096]{1,0:T(8,128)(2,1)}, u32[]{:S(2)}, u32[]{:S(2)}) %collective-permute-start.4) | collective-permute-done | bytes 2097184 | tf_op jit(solution)/shard_map/ppermute | solution.py:36
  129.4 5.7 fusion.14
  140.7 31.7 %attention_forward.1 = (f32[64,4096]{1,0:T(8,128)S(1)}, f32[1,4096]{1,0:T(1,128)S(1)}) custom-call(s32[4]{0:T(128)S(1)} %get-tuple-element.144.lo_ref, s32[4]{0:T(128)S(1)} %get-tuple-element.143.hi_ref, s32[4]{0:T(128)S(1)} %get-tuple-element.142.in_lo_ref, s32[4]{0:T(128)S(1)} %get-tuple-element.141.in_hi_ref, bf16[4096,64]{1,0:T(8,128)(2,1)S(1)} %copy-done.2, ...), custom_call_target="tpu_custom_call" | custom-call | flops 4294967296 | bytes 4194304 | tf_op jit(solution)/shard_map/attention_forward/pallas_call | solution.py:88
  173.3 6.0 all-to-all-start
  179.4 3.1 constant_dynamic-update-slice_fusion.13
  182.5 3.1 constant_dynamic-update-slice_fusion.10
  185.6 3.1 constant_dynamic-update-slice_fusion.9
  188.7 3.1 constant_dynamic-update-slice_fusion.12
  196.6 16.0 %multiply_convert_fusion = (bf16[256,4096]{1,0:T(8,128)(2,1)S(1)}, f32[256,4096]{1,0:T(8,128)}, f32[256,4096]{1,0:T(8,128)}) fusion(f32[4096]{0:T(1024)S(1)} %bitcast.339, bf16[256,1024]{1,0:T(8,128)(2,1)S(1)} %fusion.52, bf16[1024,4096]{1,0:T(8,128)(2,1)} %constant_dynamic-update-slice_fusion.12), kind=kOutput, calls=%fused_computation.24 | convolution fusion | flops 2216689664 | bytes 19415040 | tf_op jit(solution)/shard_map/dot_general | solution.py:30
  218.2 6.7 fusion.85
  225.0 7.1 %multiply_reduce_fusion = (f32[1024]{0:T(1024)S(1)}, f32[256]{0:T(256)S(1)}, f32[1024]{0:T(1024)S(1)}, f32[256,1024]{1,0:T(8,128)S(1)}) fusion(f32[256,1024]{1,0:T(8,128)S(1)} %get-tuple-element.188, f32[256]{0:T(256)S(1)} %fusion.73, f32[256]{0:T(256)S(1)} %broadcast_multiply_fusion.1, f32[1024]{0:T(1024)S(1)} %bitcast.329, ...), kind=kOutput, calls=%fused_computation.86 | convolution fusion | flops 2150102784 | bytes 13647872 | tf_op jit(solution)/shard_map/dot_general | solution.py:30
  238.3 3.1 convolution_convert_fusion.3
  241.4 4.4 all-to-all-start.1
  250.7 3.3 convolution_convert_fusion
  256.7 3.3 all-to-all-done.1
  272.6 47.6 %attention_backward.1 = (f32[4096,64]{1,0:T(8,128)}, f32[4096,64]{1,0:T(8,128)}, f32[64,4096]{1,0:T(8,128)S(1)}) custom-call(s32[8]{0:T(128)S(1)} %get-tuple-element.138.lo_ref, s32[8]{0:T(128)S(1)} %get-tuple-element.137.hi_ref, s32[8]{0:T(128)S(1)} %get-tuple-element.136.in_lo_ref, s32[8]{0:T(128)S(1)} %get-tuple-element.135.in_hi_ref, ...), custom_call_target="tpu_custom_call" | custom-call | flops 10737418240 | bytes 10485760 | tf_op jit(solution)/shard_map/attention_backward/pallas_call | solution.py:156
  325.1 3.4 collective-permute-done.18
  331.0 4.9 fusion.40
  338.6 4.1 add_convert_fusion.1
  346.8 5.7 fusion.43
  355.6 4.9 psum.7
  362.5 35.2 %collective-permute-done.26 = bf16[2,2,2,32,4096]{4,3,2,1,0:T(8,128)(2,1)} collective-permute-done((bf16[2,2,2,32,4096]{4,3,2,1,0:T(8,128)(2,1)}, bf16[2,2,2,32,4096]{4,3,2,1,0:T(8,128)(2,1)}, u32[]{:S(2)}, u32[]{:S(2)}) %collective-permute-start.26) | collective-permute-done | bytes 2097184 | tf_op jit(solution)/shard_map/ppermute | solution.py:36
  397.7 3.0 fusion.19
  401.8 4.6 reshape.338
  406.4 18.1 %collective-permute-done.27 = bf16[2,2,32,4096]{3,2,1,0:T(8,128)(2,1)} collective-permute-done((bf16[2,2,32,4096]{3,2,1,0:T(8,128)(2,1)}, bf16[2,2,32,4096]{3,2,1,0:T(8,128)(2,1)}, u32[]{:S(2)}, u32[]{:S(2)}) %collective-permute-start.27) | collective-permute-done | bytes 1048608 | tf_op jit(solution)/shard_map/ppermute | solution.py:36
  433.2 3.3 convolution_convert_fusion.1
  440.5 12.4 %collective-permute-done.29 = bf16[32,4096]{1,0:T(8,128)(2,1)S(1)} collective-permute-done((bf16[32,4096]{1,0:T(8,128)(2,1)S(1)}, bf16[32,4096]{1,0:T(8,128)(2,1)S(1)}, u32[]{:S(2)}, u32[]{:S(2)}) %collective-permute-start.29) | collective-permute-done | bytes 262176 | tf_op jit(solution)/shard_map/ppermute | solution.py:36
  455.6 3.5 add_convert_fusion
  459.6 47.3 %collective-permute-done.31 = bf16[2,2,2,128,1024]{4,3,2,1,0:T(8,128)(2,1)S(1)} collective-permute-done((bf16[2,2,2,128,1024]{4,3,2,1,0:T(8,128)(2,1)S(1)}, bf16[2,2,2,128,1024]{4,3,2,1,0:T(8,128)(2,1)S(1)}, u32[]{:S(2)}, u32[]{:S(2)}) %collective-permute-start.31) | collective-permute-done | bytes 2097184 | tf_op jit(solution)/shard_map/ppermute | solution.py:36
  508.3 23.9 %collective-permute-done.32 = bf16[2,2,128,1024]{3,2,1,0:T(8,128)(2,1)S(1)} collective-permute-done((bf16[2,2,128,1024]{3,2,1,0:T(8,128)(2,1)S(1)}, bf16[2,2,128,1024]{3,2,1,0:T(8,128)(2,1)S(1)}, u32[]{:S(2)}, u32[]{:S(2)}) %collective-permute-start.32) | collective-permute-done | bytes 1048608 | tf_op jit(solution)/shard_map/ppermute | solution.py:36
  532.8 12.1 %collective-permute-done.33 = bf16[2,128,1024]{2,1,0:T(8,128)(2,1)S(1)} collective-permute-done((bf16[2,128,1024]{2,1,0:T(8,128)(2,1)S(1)}, bf16[2,128,1024]{2,1,0:T(8,128)(2,1)S(1)}, u32[]{:S(2)}, u32[]{:S(2)}) %collective-permute-start.33) | collective-permute-done | bytes 524320 | tf_op jit(solution)/shard_map/ppermute | solution.py:36
  545.2 12.1 %collective-permute-done.34 = bf16[128,1024]{1,0:T(8,128)(2,1)S(1)} collective-permute-done((bf16[128,1024]{1,0:T(8,128)(2,1)S(1)}, bf16[128,1024]{1,0:T(8,128)(2,1)S(1)}, u32[]{:S(2)}, u32[]{:S(2)}) %collective-permute-start.34) | collective-permute-done | bytes 262176 | tf_op jit(solution)/shard_map/ppermute | solution.py:36
  570.0 5.1 collective-permute-done.12
  575.1 11.2 %collective-permute-done.10 = bf16[256,1024]{1,0:T(8,128)(2,1)} collective-permute-done((bf16[256,1024]{1,0:T(8,128)(2,1)}, bf16[256,1024]{1,0:T(8,128)(2,1)}, u32[]{:S(2)}, u32[]{:S(2)}) %collective-permute-start.10) | collective-permute-done | bytes 524320 | tf_op jit(solution)/shard_map/ppermute | solution.py:36
  586.4 9.9 %collective-permute-done.8 = bf16[256,1024]{1,0:T(8,128)(2,1)} collective-permute-done((bf16[256,1024]{1,0:T(8,128)(2,1)}, bf16[256,1024]{1,0:T(8,128)(2,1)}, u32[]{:S(2)}, u32[]{:S(2)}) %collective-permute-start.8) | collective-permute-done | bytes 524320 | tf_op jit(solution)/shard_map/ppermute | solution.py:36
  600.0 4.7 all-to-all-start.2
  618.3 13.1 %collective-permute-done.23 = f32[1,5120]{1,0:T(1,128)S(1)} collective-permute-done((f32[1,5120]{1,0:T(1,128)S(1)}, f32[1,5120]{1,0:T(1,128)S(1)}, u32[]{:S(2)}, u32[]{:S(2)}) %collective-permute-start.23) | collective-permute-done | bytes 20512 | tf_op jit(solution)/shard_map/ppermute | solution.py:36
  631.4 4.5 collective-permute-start.24
  637.8 5.4 collective-permute-done.24
  652.5 3.1 copy.132
  655.6 3.3 slice_bitcast_fusion
  670.4 6.7 copy.137
  677.1 6.7 copy.138
  (328 shorter events, 161.5 us)
Async XLA Ops:
  7.2 122.2 %all-gather.12.cloned.1.call-start = ((), (), s32[]{:S(2)}) async-start(), calls=%async_computation.3 | async-start | bytes 8912896 | tf_op jit(solution)/shard_map/all_gather | solution.py:223
  14.1 45.2 %collective-permute-start.1 = (bf16[1,6144]{1,0:T(2,128)(2,1)S(1)}, bf16[1,6144]{1,0:T(2,128)(2,1)S(1)}, u32[]{:S(2)}, u32[]{:S(2)}) collective-permute-start(bf16[1,6144]{1,0:T(2,128)(2,1)S(1)} %broadcast_in_dim.16), channel_id=1, source_target_pairs={{0,1},{1,0},{2,3},{3,2},{4,5},{5,4},{6,7},{7,6},{8,9},{9,8},{10,11... | collective-permute-start | bytes 36872 | tf_op jit(solution)/shard_map/ppermute | solution.py:36
  20.4 39.5 %collective-permute-start = (bf16[512,192]{1,0:T(8,128)(2,1)S(1)}, bf16[512,192]{1,0:T(8,128)(2,1)}, u32[]{:S(2)}, u32[]{:S(2)}) collective-permute-start(bf16[512,192]{1,0:T(8,128)(2,1)S(1)} %pad_maximum_fusion.2), channel_id=1, source_target_pairs={{0,1},{1,0},{2,3},{3,2},{4,5},{5,4},{6,7},{7,6},{8,9},{9,8},{10,11... | collective-permute-start | bytes 589832 | tf_op jit(solution)/shard_map/ppermute | solution.py:36
  22.4 37.2 %collective-permute-start.2 = (bf16[256,1024]{1,0:T(8,128)(2,1)}, bf16[256,1024]{1,0:T(8,128)(2,1)S(1)}, u32[]{:S(2)}, u32[]{:S(2)}) collective-permute-start(bf16[256,1024]{1,0:T(8,128)(2,1)} %constant_dynamic-slice_fusion.11), channel_id=1, source_target_pairs={{0,1},{1,0},{2,3},{3,2},{4,5},{5,4},{6,7},{7,6},{8,9},{9,8},{10,11... | collective-permute-start | bytes 1572872 | tf_op jit(solution)/shard_map/ppermute | solution.py:36
  27.6 58.3 %collective-permute-start.6 = (bf16[1024,1024]{1,0:T(8,128)(2,1)}, bf16[1024,1024]{1,0:T(8,128)(2,1)}, u32[]{:S(2)}, u32[]{:S(2)}) collective-permute-start(bf16[1024,1024]{1,0:T(8,128)(2,1)} %constant_dynamic-slice_fusion.9), channel_id=1, source_target_pairs={{0,1},{1,0},{2,3},{3,2},{4,5},{5,4},{6,7},{7,6},{8,9},{9,8},{10,11... | collective-permute-start | bytes 6291464 | tf_op jit(solution)/shard_map/ppermute | solution.py:36
  29.1 100.3 %collective-permute-start.4 = (bf16[256,4096]{1,0:T(8,128)(2,1)}, bf16[256,4096]{1,0:T(8,128)(2,1)}, u32[]{:S(2)}, u32[]{:S(2)}) collective-permute-start(bf16[256,4096]{1,0:T(8,128)(2,1)} %constant_dynamic-slice_fusion.10), channel_id=1, source_target_pairs={{0,1},{1,0},{2,3},{3,2},{4,5},{5,4},{6,7},{7,6},{8,9},{9,8},{10,11... | collective-permute-start | bytes 6291464 | tf_op jit(solution)/shard_map/ppermute | solution.py:36
  59.6 2.3 collective-permute-start.3
  61.9 67.5 %copy-start.15 = (bf16[1024,1024]{1,0:T(8,128)(2,1)}, bf16[1024,1024]{1,0:T(8,128)(2,1)S(1)}, u32[]{:S(2)}) copy-start(bf16[1024,1024]{1,0:T(8,128)(2,1)S(1)} %constant_dynamic-update-slice_fusion.15) | copy-start | bytes 6291460
  85.9 99.7 %collective-permute-start.7 = (bf16[1024,1024]{1,0:T(8,128)(2,1)}, bf16[1024,1024]{1,0:T(8,128)(2,1)}, u32[]{:S(2)}, u32[]{:S(2)}) collective-permute-start(bf16[1024,1024]{1,0:T(8,128)(2,1)} %collective-permute-done.6), channel_id=1, source_target_pairs={{0,2},{2,0},{4,6},{6,4},{8,10},{10,8},{12,14},{14,12},{16,18},{18,... | collective-permute-start | bytes 6291464 | tf_op jit(solution)/shard_map/ppermute | solution.py:36
  129.4 59.3 %collective-permute-start.5 = (bf16[256,4096]{1,0:T(8,128)(2,1)}, bf16[256,4096]{1,0:T(8,128)(2,1)}, u32[]{:S(2)}, u32[]{:S(2)}) collective-permute-start(bf16[256,4096]{1,0:T(8,128)(2,1)} %collective-permute-done.4), channel_id=1, source_target_pairs={{0,2},{2,0},{4,6},{6,4},{8,10},{10,8},{12,14},{14,12},{16,18},{18,... | collective-permute-start | bytes 6291464 | tf_op jit(solution)/shard_map/ppermute | solution.py:36
  137.3 35.1 %copy-start = (bf16[4096,64]{1,0:T(8,128)(2,1)}, bf16[4096,64]{1,0:T(8,128)(2,1)S(1)}, u32[]{:S(2)}) copy-start(bf16[4096,64]{1,0:T(8,128)(2,1)S(1)} %get-tuple-element.155.k_ref) | copy-start | bytes 1572868
  173.3 20.3 %all-to-all-start = ((bf16[16,64,256]{2,1,0:T(8,128)(2,1)}), bf16[16,64,256]{2,1,0:T(8,128)(2,1)S(1)}, u32[]{:S(2)}, u32[]{:S(2)}) async-start(bf16[16,64,256]{2,1,0:T(8,128)(2,1)} %bitcast.281), calls=%async_computation | async-start | bytes 1048576 | tf_op jit(solution)/shard_map/all_to_all | solution.py:254
  235.8 11.3 %collective-permute-start.15 = (bf16[512,1024]{1,0:T(8,128)(2,1)}, bf16[512,1024]{1,0:T(8,128)(2,1)}, u32[]{:S(2)}, u32[]{:S(2)}) collective-permute-start(bf16[512,1024]{1,0:T(8,128)(2,1)} %convolution_convert_fusion.2), channel_id=1, source_target_pairs={{0,2},{2,0},{4,6},{6,4},{8,10},{10,8},{12,14},{14,12},{16,18},{18,... | collective-permute-start | bytes 3145736 | tf_op jit(solution)/shard_map/ppermute | solution.py:36
  241.4 18.7 %all-to-all-start.1 = ((bf16[16,64,256]{2,1,0:T(8,128)(2,1)}), bf16[16,64,256]{2,1,0:T(8,128)(2,1)S(1)}, u32[]{:S(2)}, u32[]{:S(2)}) async-start(bf16[16,64,256]{2,1,0:T(8,128)(2,1)} %bitcast.322), calls=%async_computation.1 | async-start | bytes 1048576 | tf_op jit(solution)/shard_map/all_to_all | solution.py:275
  245.8 403.9 %all-gather.14.cloned.1.call-start = ((), (), s32[]{:S(2)}) async-start(), calls=%async_computation.4 | async-start | bytes 1114112 | tf_op jit(solution)/shard_map/all_gather | solution.py:309
  250.7 14.6 %collective-permute-start.16 = (bf16[2,2,2,32,1024]{4,3,2,1,0:T(8,128)(2,1)}, bf16[2,2,2,32,1024]{4,3,2,1,0:T(8,128)(2,1)}, u32[]{:S(2)}, u32[]{:S(2)}) collective-permute-start(bf16[2,2,2,32,1024]{4,3,2,1,0:T(8,128)(2,1)} %dynamic-slice_bitcast_fusion.6), channel_id=1, source_target_pairs={{0,1},{1,0},{2,3},{3,2},{4,5},{5,4},{6,7},{7,6},{8,9},{9,8},{10,11... | collective-permute-start | bytes 1572872 | tf_op jit(solution)/shard_map/ppermute | solution.py:36
  254.0 84.7 %collective-permute-start.25 = (bf16[512,4096]{1,0:T(8,128)(2,1)}, bf16[512,4096]{1,0:T(8,128)(2,1)}, u32[]{:S(2)}, u32[]{:S(2)}) collective-permute-start(bf16[512,4096]{1,0:T(8,128)(2,1)} %convolution_convert_fusion), channel_id=1, source_target_pairs={{0,2},{2,0},{4,6},{6,4},{8,10},{10,8},{12,14},{14,12},{16,18},{18,... | collective-permute-start | bytes 12582920 | tf_op jit(solution)/shard_map/ppermute | solution.py:36
  267.4 54.9 %collective-permute-start.17 = (bf16[2,2,32,1024]{3,2,1,0:T(8,128)(2,1)}, bf16[2,2,32,1024]{3,2,1,0:T(8,128)(2,1)}, u32[]{:S(2)}, u32[]{:S(2)}) collective-permute-start(bf16[2,2,32,1024]{3,2,1,0:T(8,128)(2,1)} %dynamic-slice_bitcast_fusion.9), channel_id=1, source_target_pairs={{0,4},{2,6},{4,0},{6,2},{8,12},{10,14},{12,8},{14,10},{16,20},{18,... | collective-permute-start | bytes 786440 | tf_op jit(solution)/shard_map/ppermute | solution.py:36
  323.5 5.0 collective-permute-start.18
  328.6 9.3 %collective-permute-start.19 = (bf16[32,1024]{1,0:T(8,128)(2,1)S(1)}, bf16[32,1024]{1,0:T(8,128)(2,1)S(1)}, u32[]{:S(2)}, u32[]{:S(2)}) collective-permute-start(bf16[32,1024]{1,0:T(8,128)(2,1)S(1)} %dynamic-slice_bitcast_fusion.11), channel_id=1, source_target_pairs={{0,16},{2,18},{4,20},{6,22},{8,24},{10,26},{12,28},{14,30},{16,0},... | collective-permute-start | bytes 196616 | tf_op jit(solution)/shard_map/ppermute | solution.py:36
  338.6 313.9 %all-gather.20.cloned.1.call-start = ((), (), s32[]{:S(2)}) async-start(), calls=%async_computation.7 | async-start | bytes 4177920 | tf_op jit(solution)/shard_map/all_gather | solution.py:368
  346.2 51.5 %collective-permute-start.26 = (bf16[2,2,2,32,4096]{4,3,2,1,0:T(8,128)(2,1)}, bf16[2,2,2,32,4096]{4,3,2,1,0:T(8,128)(2,1)}, u32[]{:S(2)}, u32[]{:S(2)}) collective-permute-start(bf16[2,2,2,32,4096]{4,3,2,1,0:T(8,128)(2,1)} %dynamic-slice_bitcast_fusion.1), channel_id=1, source_target_pairs={{0,4},{2,6},{4,0},{6,2},{8,12},{10,14},{12,8},{14,10},{16,20},{18,... | collective-permute-start | bytes 6291464 | tf_op jit(solution)/shard_map/ppermute | solution.py:36
  354.3 6.3 collective-permute-start.14
  362.5 308.0 %all-gather.16.cloned.1.call-start = ((), (), s32[]{:S(2)}) async-start(), calls=%async_computation.5 | async-start | bytes 4456448 | tf_op jit(solution)/shard_map/all_gather | solution.py:309
  401.8 22.7 %collective-permute-start.27 = (bf16[2,2,32,4096]{3,2,1,0:T(8,128)(2,1)}, bf16[2,2,32,4096]{3,2,1,0:T(8,128)(2,1)}, u32[]{:S(2)}, u32[]{:S(2)}) collective-permute-start(bf16[2,2,32,4096]{3,2,1,0:T(8,128)(2,1)} %dynamic-slice_bitcast_fusion.3), channel_id=1, source_target_pairs={{0,1},{1,0},{2,3},{3,2},{4,5},{5,4},{6,7},{7,6},{8,9},{9,8},{10,11... | collective-permute-start | bytes 3145736 | tf_op jit(solution)/shard_map/ppermute | solution.py:36
  426.9 10.5 %collective-permute-start.28 = (bf16[2,32,4096]{2,1,0:T(8,128)(2,1)S(1)}, bf16[2,32,4096]{2,1,0:T(8,128)(2,1)}, u32[]{:S(2)}, u32[]{:S(2)}) collective-permute-start(bf16[2,32,4096]{2,1,0:T(8,128)(2,1)S(1)} %dynamic-slice_bitcast_fusion.5), channel_id=1, source_target_pairs={{0,8},{2,10},{4,12},{6,14},{8,0},{10,2},{12,4},{14,6},{16,24},{18,... | collective-permute-start | bytes 1572872 | tf_op jit(solution)/shard_map/ppermute | solution.py:36
  436.5 19.1 %collective-permute-start.30 = (bf16[2048,1024]{1,0:T(8,128)(2,1)}, bf16[2048,1024]{1,0:T(8,128)(2,1)}, u32[]{:S(2)}, u32[]{:S(2)}) collective-permute-start(bf16[2048,1024]{1,0:T(8,128)(2,1)} %convolution_convert_fusion.1), channel_id=1, source_target_pairs={{0,2},{2,0},{4,6},{6,4},{8,10},{10,8},{12,14},{14,12},{16,18},{18,... | collective-permute-start | bytes 12582920 | tf_op jit(solution)/shard_map/ppermute | solution.py:36
  438.6 14.3 %collective-permute-start.29 = (bf16[32,4096]{1,0:T(8,128)(2,1)S(1)}, bf16[32,4096]{1,0:T(8,128)(2,1)S(1)}, u32[]{:S(2)}, u32[]{:S(2)}) collective-permute-start(bf16[32,4096]{1,0:T(8,128)(2,1)S(1)} %dynamic-slice_bitcast_fusion.8), channel_id=1, source_target_pairs={{0,16},{2,18},{4,20},{6,22},{8,24},{10,26},{12,28},{14,30},{16,0},... | collective-permute-start | bytes 786440 | tf_op jit(solution)/shard_map/ppermute | solution.py:36
  453.7 223.4 %all-gather.18.cloned.1.call-start = ((), (), s32[]{:S(2)}) async-start(), calls=%async_computation.6 | async-start | bytes 4456448 | tf_op jit(solution)/shard_map/all_gather | solution.py:309
  459.3 47.6 %collective-permute-start.31 = (bf16[2,2,2,128,1024]{4,3,2,1,0:T(8,128)(2,1)S(1)}, bf16[2,2,2,128,1024]{4,3,2,1,0:T(8,128)(2,1)S(1)}, u32[]{:S(2)}, u32[]{:S(2)}) collective-permute-start(bf16[2,2,2,128,1024]{4,3,2,1,0:T(8,128)(2,1)S(1)} %dynamic-slice_bitcast_fusion), channel_id=1, source_target_pairs={{0,1},{1,0},{2,3},{3,2},{4,5},{5,4},{6,7},{7,6},{8,9},{9,8},{10,11... | collective-permute-start | bytes 6291464 | tf_op jit(solution)/shard_map/ppermute | solution.py:36
  507.9 24.3 %collective-permute-start.32 = (bf16[2,2,128,1024]{3,2,1,0:T(8,128)(2,1)S(1)}, bf16[2,2,128,1024]{3,2,1,0:T(8,128)(2,1)S(1)}, u32[]{:S(2)}, u32[]{:S(2)}) collective-permute-start(bf16[2,2,128,1024]{3,2,1,0:T(8,128)(2,1)S(1)} %dynamic-slice_bitcast_fusion.2), channel_id=1, source_target_pairs={{0,4},{2,6},{4,0},{6,2},{8,12},{10,14},{12,8},{14,10},{16,20},{18,... | collective-permute-start | bytes 3145736 | tf_op jit(solution)/shard_map/ppermute | solution.py:36
  532.6 33.5 %copy-start.26 = (bf16[1,256,1024]{2,1,0:T(8,128)(2,1)S(1)}, bf16[1,256,1024]{2,1,0:T(8,128)(2,1)}, u32[]{:S(2)}) copy-start(bf16[1,256,1024]{2,1,0:T(8,128)(2,1)} %param.35) | copy-start | bytes 1572868
  532.7 12.2 %collective-permute-start.33 = (bf16[2,128,1024]{2,1,0:T(8,128)(2,1)S(1)}, bf16[2,128,1024]{2,1,0:T(8,128)(2,1)S(1)}, u32[]{:S(2)}, u32[]{:S(2)}) collective-permute-start(bf16[2,128,1024]{2,1,0:T(8,128)(2,1)S(1)} %dynamic-slice_bitcast_fusion.4), channel_id=1, source_target_pairs={{0,8},{2,10},{4,12},{6,14},{8,0},{10,2},{12,4},{14,6},{16,24},{18,... | collective-permute-start | bytes 1572872 | tf_op jit(solution)/shard_map/ppermute | solution.py:36
  545.1 12.2 %collective-permute-start.34 = (bf16[128,1024]{1,0:T(8,128)(2,1)S(1)}, bf16[128,1024]{1,0:T(8,128)(2,1)S(1)}, u32[]{:S(2)}, u32[]{:S(2)}) collective-permute-start(bf16[128,1024]{1,0:T(8,128)(2,1)S(1)} %dynamic-slice_bitcast_fusion.7), channel_id=1, source_target_pairs={{0,16},{2,18},{4,20},{6,22},{8,24},{10,26},{12,28},{14,30},{16,0},... | collective-permute-start | bytes 786440 | tf_op jit(solution)/shard_map/ppermute | solution.py:36
  560.0 15.1 %collective-permute-start.12 = (bf16[256,1024]{1,0:T(8,128)(2,1)}, bf16[256,1024]{1,0:T(8,128)(2,1)}, u32[]{:S(2)}, u32[]{:S(2)}) collective-permute-start(bf16[256,1024]{1,0:T(8,128)(2,1)} %constant_dynamic-slice_fusion.6), channel_id=1, source_target_pairs={{0,1},{1,0},{2,3},{3,2},{4,5},{5,4},{6,7},{7,6},{8,9},{9,8},{10,11... | collective-permute-start | bytes 1572872 | tf_op jit(solution)/shard_map/ppermute | solution.py:36
  562.2 24.1 %collective-permute-start.10 = (bf16[256,1024]{1,0:T(8,128)(2,1)}, bf16[256,1024]{1,0:T(8,128)(2,1)}, u32[]{:S(2)}, u32[]{:S(2)}) collective-permute-start(bf16[256,1024]{1,0:T(8,128)(2,1)} %constant_dynamic-slice_fusion.7), channel_id=1, source_target_pairs={{0,1},{1,0},{2,3},{3,2},{4,5},{5,4},{6,7},{7,6},{8,9},{9,8},{10,11... | collective-permute-start | bytes 1572872 | tf_op jit(solution)/shard_map/ppermute | solution.py:36
  565.8 30.5 %collective-permute-start.8 = (bf16[256,1024]{1,0:T(8,128)(2,1)}, bf16[256,1024]{1,0:T(8,128)(2,1)}, u32[]{:S(2)}, u32[]{:S(2)}) collective-permute-start(bf16[256,1024]{1,0:T(8,128)(2,1)} %constant_dynamic-slice_fusion.8), channel_id=1, source_target_pairs={{0,1},{1,0},{2,3},{3,2},{4,5},{5,4},{6,7},{7,6},{8,9},{9,8},{10,11... | collective-permute-start | bytes 1572872 | tf_op jit(solution)/shard_map/ppermute | solution.py:36
  569.6 27.8 %copy-start.16 = (bf16[1024,1024]{1,0:T(8,128)(2,1)}, bf16[1024,1024]{1,0:T(8,128)(2,1)S(1)}, u32[]{:S(2)}) copy-start(bf16[1024,1024]{1,0:T(8,128)(2,1)S(1)} %constant_dynamic-update-slice_fusion.2) | copy-start | bytes 6291460
  570.0 27.4 %copy-start.20 = (bf16[1024,1024]{1,0:T(8,128)(2,1)}, bf16[1024,1024]{1,0:T(8,128)(2,1)S(1)}, u32[]{:S(2)}) copy-start(bf16[1024,1024]{1,0:T(8,128)(2,1)S(1)} %constant_dynamic-update-slice_fusion.8) | copy-start | bytes 6291460
  575.1 41.3 %collective-permute-start.13 = (bf16[256,1024]{1,0:T(8,128)(2,1)}, bf16[256,1024]{1,0:T(8,128)(2,1)}, u32[]{:S(2)}, u32[]{:S(2)}) collective-permute-start(bf16[256,1024]{1,0:T(8,128)(2,1)} %collective-permute-done.12), channel_id=1, source_target_pairs={{0,2},{2,0},{4,6},{6,4},{8,10},{10,8},{12,14},{14,12},{16,18},{18,... | collective-permute-start | bytes 1572872 | tf_op jit(solution)/shard_map/ppermute | solution.py:36
  586.4 26.2 %collective-permute-start.11 = (bf16[256,1024]{1,0:T(8,128)(2,1)}, bf16[256,1024]{1,0:T(8,128)(2,1)}, u32[]{:S(2)}, u32[]{:S(2)}) collective-permute-start(bf16[256,1024]{1,0:T(8,128)(2,1)} %collective-permute-done.10), channel_id=1, source_target_pairs={{0,2},{2,0},{4,6},{6,4},{8,10},{10,8},{12,14},{14,12},{16,18},{18,... | collective-permute-start | bytes 1572872 | tf_op jit(solution)/shard_map/ppermute | solution.py:36
  596.3 39.6 %collective-permute-start.9 = (bf16[256,1024]{1,0:T(8,128)(2,1)}, bf16[256,1024]{1,0:T(8,128)(2,1)}, u32[]{:S(2)}, u32[]{:S(2)}) collective-permute-start(bf16[256,1024]{1,0:T(8,128)(2,1)} %collective-permute-done.8), channel_id=1, source_target_pairs={{0,2},{2,0},{4,6},{6,4},{8,10},{10,8},{12,14},{14,12},{16,18},{18,... | collective-permute-start | bytes 1572872 | tf_op jit(solution)/shard_map/ppermute | solution.py:36
  600.0 44.4 %all-to-all-start.2 = ((bf16[16,256,192]{1,2,0:T(8,128)(2,1)}), bf16[16,256,192]{1,2,0:T(8,128)(2,1)}, u32[]{:S(2)}, u32[]{:S(2)}) async-start(bf16[16,256,192]{1,2,0:T(8,128)(2,1)} %bitcast.301), calls=%async_computation.2 | async-start | bytes 3145728 | tf_op jit(solution)/shard_map/all_to_all | solution.py:348
  604.7 3.8 collective-permute-start.20
  608.6 2.0 collective-permute-start.21
  610.6 4.9 collective-permute-start.22
  615.5 15.9 %collective-permute-start.23 = (f32[1,5120]{1,0:T(1,128)S(1)}, f32[1,5120]{1,0:T(1,128)S(1)}, u32[]{:S(2)}, u32[]{:S(2)}) collective-permute-start(f32[1,5120]{1,0:T(1,128)S(1)} %add.431), channel_id=1, source_target_pairs={{0,8},{2,10},{4,12},{6,14},{8,0},{10,2},{12,4},{14,6},{16,24},{18,... | collective-permute-start | bytes 61448 | tf_op jit(solution)/shard_map/ppermute | solution.py:36
  631.4 11.8 %collective-permute-start.24 = (f32[1,5120]{1,0:T(1,128)S(1)}, f32[1,5120]{1,0:T(1,128)S(1)}, u32[]{:S(2)}, u32[]{:S(2)}) collective-permute-start(f32[1,5120]{1,0:T(1,128)S(1)} %add.432), channel_id=1, source_target_pairs={{0,16},{2,18},{4,20},{6,22},{8,24},{10,26},{12,28},{14,30},{16,0},... | collective-permute-start | bytes 61448 | tf_op jit(solution)/shard_map/ppermute | solution.py:36
  (38 other events, 186.7 us)
Sparse Core Ops, SparseCore 0:
  10.2 77.1 all-gather.11
  338.7 37.5 all-gather.13
  378.6 48.8 all-gather.19
  453.8 47.2 all-gather.15
  558.3 46.6 all-gather.17

commit v2 on v1

v2 whole, which is shorter than its diff:
```python
import functools
import math

import jax
import jax.numpy as jnp
from jax import lax
from jax.experimental import pallas as pl
from jax.experimental.pallas import tpu as pltpu
from jax.sharding import PartitionSpec as P

HEADS = 16
LOG2E = 1.4426950408889634
NEG = -1e30
BF = jnp.bfloat16
F32 = jnp.float32


def layer_norm(hidden, gain, shift):
    mean = jnp.mean(hidden, axis=-1, keepdims=True)
    centred = hidden - mean
    variance = jnp.mean(centred * centred, axis=-1, keepdims=True)
    return centred * lax.rsqrt(variance + 1e-05) * gain + shift


def gelu_exact(value):
    return jax.nn.gelu(value, approximate=False)


def dot(left, right, on_left, on_right):
    return lax.dot_general(
        left, right, (((on_left,), (on_right,)), ((), ())), preferred_element_type=F32
    )


def flip(value, axis, bit, size):
    return lax.ppermute(value, axis, [(i, i ^ bit) for i in range(size)])


def forward_kernel(
    lo_ref, hi_ref, in_lo_ref, in_hi_ref, q_ref, k_ref, vt_ref, start_ref, end_ref,
    out_ref, lse_ref, total_ref, *, bk, scale
):
    i = pl.program_id(0)
    bq = q_ref.shape[0]
    q = q_ref[...]
    start, end = start_ref[...], end_ref[...]
    total_ref[...] = jnp.zeros_like(total_ref)

    def step(j, carry, masked):
        peak, norm = carry
        at = pl.multiple_of(j * bk, bk)
        s = dot(k_ref[pl.ds(at, bk), :], q, 1, 1) * (scale * LOG2E)
        if masked:
            at_key = lax.broadcasted_iota(jnp.int32, (bk, bq), 0) + at
            s = jnp.where((at_key >= start) & (at_key < end), s, NEG)
        new_peak = jnp.maximum(peak, jnp.max(s, axis=0, keepdims=True))
        p = jnp.exp2(s - new_peak)
        shrink = jnp.exp2(peak - new_peak)
        norm = norm * shrink + jnp.sum(p, axis=0, keepdims=True)
        total_ref[...] = total_ref[...] * shrink + dot(vt_ref[:, pl.ds(at, bk)], p.astype(BF), 1, 0)
        return new_peak, norm

    lo, hi, in_lo, in_hi = lo_ref[i], hi_ref[i], in_lo_ref[i], in_hi_ref[i]
    carry = (jnp.full((1, bq), NEG, F32), jnp.zeros((1, bq), F32))
    carry = lax.fori_loop(in_lo, in_hi, lambda j, c: step(j, c, False), carry)
    carry = lax.fori_loop(lo, in_lo, lambda j, c: step(j, c, True), carry)
    peak, norm = lax.fori_loop(in_hi, hi, lambda j, c: step(j, c, True), carry)
    out_ref[...] = total_ref[...] / norm
    lse_ref[...] = peak + jnp.log2(norm)


def block_ranges(starts, ends, rows, others):
    first, last = starts.reshape(-1, rows), ends.reshape(-1, rows)
    lo = first[:, 0] // others
    hi = (last[:, -1] + others - 1) // others
    in_lo = jnp.clip((first[:, -1] + others - 1) // others, lo, hi)
    in_hi = jnp.clip(last[:, 0] // others, in_lo, hi)
    return lo, hi, in_lo, in_hi


def attention_forward(q, k, vt, starts, ends, scale, bq=1024, bk=512):
    count, d = q.shape
    length = k.shape[0]
    bq = min(bq, count)
    ranges = block_ranges(starts, ends, bq, bk)
    row = lambda: pl.BlockSpec((1, bq), lambda i, *_: (0, i))
    whole = lambda shape: pl.BlockSpec(shape, lambda i, *_: (0, 0))
    return pl.pallas_call(
        functools.partial(forward_kernel, bk=bk, scale=scale),
        out_shape=(
            jax.ShapeDtypeStruct((d, count), F32),
            jax.ShapeDtypeStruct((1, count), F32),
        ),
        grid_spec=pltpu.PrefetchScalarGridSpec(
            num_scalar_prefetch=4,
            grid=(count // bq,),
            in_specs=[
                pl.BlockSpec((bq, d), lambda i, *_: (i, 0)),
                whole((length, d)),
                whole((d, length)),
                row(),
                row(),
            ],
            out_specs=[pl.BlockSpec((d, bq), lambda i, *_: (0, i)), row()],
            scratch_shapes=[pltpu.VMEM((d, bq), F32)],
        ),
        compiler_params=pltpu.CompilerParams(vmem_limit_bytes=40 << 20),
        cost_estimate=pl.CostEstimate(
            flops=4 * count * length * d, bytes_accessed=length * d * 16, transcendentals=count * length
        ),
        name="attention_forward",
    )(*ranges, q, k, vt, starts[None], ends[None])


def backward_kernel(
    lo_ref, hi_ref, in_lo_ref, in_hi_ref, k_ref, v_ref, kt_ref, q_ref, do_ref, lse_ref, delta_ref, start_ref,
    end_ref, dqt_in_ref, dk_ref, dv_ref, dqt_ref, dk_sum, dv_sum, *, bq, scale, base
):
    j = pl.program_id(0) + base
    bk = k_ref.shape[0]

    @pl.when(pl.program_id(0) == 0)
    def _():
        dqt_ref[...] = dqt_in_ref[...]

    k, v, kt = k_ref[...], v_ref[...], kt_ref[...]
    dk_sum[...] = jnp.zeros_like(dk_sum)
    dv_sum[...] = jnp.zeros_like(dv_sum)

    def step(i, masked):
        at = pl.multiple_of(i * bq, bq)
        row = pl.ds(at, bq)
        q, do = q_ref[row, :], do_ref[row, :]
        s = dot(k, q, 1, 1) * (scale * LOG2E) - lse_ref[:, row]
        if masked:
            at_key = lax.broadcasted_iota(jnp.int32, (bk, bq), 0) + j * bk
            s = jnp.where((at_key >= start_ref[:, row]) & (at_key < end_ref[:, row]), s, NEG)
        p = jnp.exp2(s)
        dp = dot(v, do, 1, 1)
        dv_sum[...] += dot(p.astype(BF), do, 1, 0)
        ds = (p * (dp - delta_ref[:, row])).astype(BF)
        dk_sum[...] += dot(ds, q, 1, 0)
        dqt_ref[:, row] += dot(kt, ds, 1, 0)

    lo, hi, in_lo, in_hi = lo_ref[j], hi_ref[j], in_lo_ref[j], in_hi_ref[j]
    pl.loop(in_lo, in_hi)(lambda i: step(i, False))
    pl.loop(lo, in_lo)(lambda i: step(i, True))
    pl.loop(in_hi, hi)(lambda i: step(i, True))
    dk_ref[...] = (dk_sum[...] * scale).astype(dk_ref.dtype)
    dv_ref[...] = dv_sum[...].astype(dv_ref.dtype)


def attention_backward(q, k, v, kt, do, lse, delta, starts, ends, ranges, dqt, scale, bq, bk, base, blocks):
    count, d = q.shape
    whole = lambda shape: pl.BlockSpec(shape, lambda j, *_: (0, 0))
    keys = lambda at: pl.BlockSpec((bk, d), lambda j, *_: (j + at, 0))
    return pl.pallas_call(
        functools.partial(backward_kernel, bq=bq, scale=scale, base=base),
        out_shape=(
            jax.ShapeDtypeStruct((blocks * bk, d), BF),
            jax.ShapeDtypeStruct((blocks * bk, d), BF),
            jax.ShapeDtypeStruct((d, count), F32),
        ),
        grid_spec=pltpu.PrefetchScalarGridSpec(
            num_scalar_prefetch=4,
            grid=(blocks,),
            in_specs=[
                keys(base),
                keys(base),
                pl.BlockSpec((d, bk), lambda j, *_: (0, j + base)),
                whole((count, d)),
                whole((count, d)),
                whole((1, count)),
                whole((1, count)),
                whole((1, count)),
                whole((1, count)),
                whole((d, count)),
            ],
            out_specs=[keys(0), keys(0), whole((d, count))],
            scratch_shapes=[pltpu.VMEM((bk, d), F32), pltpu.VMEM((bk, d), F32)],
        ),
        compiler_params=pltpu.CompilerParams(vmem_limit_bytes=32 << 20),
        cost_estimate=pl.CostEstimate(
            flops=40 * count * blocks * bk * d, bytes_accessed=count * d * 24, transcendentals=count * blocks * bk
        ),
        name="attention_backward",
    )(*ranges, k, v, kt, q, do, lse, delta, starts[None], ends[None], dqt)


def body(ctx, fsdp, tokens, segments, w_query, w_key, w_value, w_out, b_query, b_value, b_out, gain_one, shift_one,
         w_up, b_up, w_down, b_down, gain_two, shift_two, cotangent):
    _, block, width = tokens.shape
    heads = HEADS
    d = width // heads
    scale = 1.0 / math.sqrt(d)
    parts = ctx // heads
    mine = block // parts
    length = ctx * block
    count = length // parts
    hidden = w_up.shape[1]
    shard = w_query.shape[0]
    me = lax.axis_index("ctx")
    row = lax.axis_index("fsdp")
    head, part = me // parts, me % parts
    core = me % 2
    cut = lambda a, at, size, axis: lax.dynamic_slice_in_dim(a, at, size, axis)

    bits = lambda n: [1 << i for i in range(n.bit_length() - 1)]
    sizes = {"fsdp": fsdp, "ctx": ctx}
    tie = lambda *arrays: lax.optimization_barrier(arrays)

    def gather_small(a):
        if fsdp == 2:
            other = flip(a, "fsdp", 1, 2)
            return jnp.concatenate([jnp.where(row == 0, a, other), jnp.where(row == 0, other, a)], axis=0)
        return lax.all_gather(a, "fsdp", axis=0, tiled=True)

    def near_half(w):
        if fsdp != 2:
            return lax.all_gather(w, "fsdp", axis=0, tiled=True)
        return flip(cut(w, core * (w.shape[0] // 2), w.shape[0] // 2, 0), "fsdp", 1, 2)

    def far_half(near):
        return flip(near, "ctx", 1, ctx) if fsdp == 2 else near

    def assemble(w, near, far):
        if fsdp != 2:
            return near
        rows, half = w.shape[0], w.shape[0] // 2
        whole = jnp.zeros((2 * rows, w.shape[1]), w.dtype)
        whole = lax.dynamic_update_slice_in_dim(whole, w, row * rows, 0)
        whole = lax.dynamic_update_slice_in_dim(whole, near, (1 - row) * rows + core * half, 0)
        return lax.dynamic_update_slice_in_dim(whole, far, (1 - row) * rows + (1 - core) * half, 0)

    def halves_of(place):
        return [("fsdp", b) for b in reversed(bits(fsdp))] + [("ctx", b) for b in bits(ctx)] if place is None else place

    def begin(left, right, step):
        axis, bit = step
        place = halves_of(None)
        at = place.index(step)
        split = left.reshape([left.shape[0]] + [2] * len(place) + [-1])
        own = (lax.axis_index(axis) // bit) % 2
        pick = lambda which: lax.dynamic_index_in_dim(split, which, at + 1, keepdims=False).reshape(left.shape[0], -1)
        sent = dot(pick(1 - own), right, 0, 0).astype(BF)
        return sent, lambda left_kept, received: (
            dot(left_kept, right, 0, 0) + received.astype(F32)
        ).astype(BF), pick(own)

    def split_step(total, place, step):
        axis, bit = step
        at = place.index(step)
        own = (lax.axis_index(axis) // bit) % 2
        keep = lax.dynamic_index_in_dim(total, own, at, keepdims=False)
        send = lax.dynamic_index_in_dim(total, 1 - own, at, keepdims=False)
        return keep, send, [p for p in place if p != step]

    def move(send, step):
        return flip(send, step[0], step[1], sizes[step[0]])

    def add(keep, received):
        return (keep.astype(F32) + received.astype(F32)).astype(BF)

    def spread(total, rows, columns):
        every = lax.all_gather(total, "ctx", axis=0, tiled=False)
        n = len(bits(ctx))
        every = every.reshape([2] * n + [-1, columns])
        every = every.transpose(list(reversed(range(n))) + [n, n + 1])
        return every.reshape(rows, columns)

    inputs = tokens[0]
    slices = jnp.concatenate([cut(w, head * d, d, 1) for w in (w_query, w_key, w_value)], axis=1)
    small = jnp.stack([b_query, b_value, b_out, gain_one, shift_one, b_down, gain_two, shift_two])
    small = jnp.concatenate([small.reshape(-1), b_up])[None]
    inputs, slices, small = tie(inputs, slices, small)
    everyone = lax.all_gather(inputs, "ctx", axis=0, tiled=True)
    w_head = gather_small(slices)
    small = gather_small(small)
    wo_near = near_half(w_out)
    wu_near = near_half(w_up)
    wo_near, w_down, w_head, small = tie(wo_near, w_down, w_head, small)
    wo = assemble(w_out, wo_near, far_half(wo_near))
    wd_near = near_half(w_down)
    wu_near, w_query, w_key, w_value, wo = tie(wu_near, w_query, w_key, w_value, wo)
    wu = assemble(w_up, wu_near, far_half(wu_near))
    wqkv = jnp.concatenate([w_query, w_key, w_value], axis=1)
    wqkv_near = near_half(wqkv)
    everyone, wu, wo = tie(everyone, wu, wo)

    eight = small[:, : 8 * shard].reshape(-1, 8, shard).transpose(1, 0, 2).reshape(8, width).astype(F32)
    bq_, bv_, bo, gain1, shift1, bd, gain2, shift2 = (eight[i] for i in range(8))
    bu = small[:, 8 * shard :].reshape(hidden).astype(F32)
    projected = dot(everyone, w_head, 1, 0)
    my_bias = jnp.concatenate([cut(bq_, head * d, d, 0), jnp.zeros((d,), F32), cut(bv_, head * d, d, 0)])
    projected = (projected + my_bias).astype(BF)
    own_part = lambda a: cut(a.reshape((ctx, block) + a.shape[1:]), part * mine, mine, 1).reshape(
        (count,) + a.shape[1:]
    )
    q = own_part(projected[:, :d])
    k, v = projected[:, d : 2 * d], projected[:, 2 * d :]
    kt, vt = k.T, v.T
    seg = segments[0]
    starts_all = jnp.sum(seg[None, :] < seg[:, None], axis=1, dtype=jnp.int32)
    ends_all = jnp.sum(seg[None, :] <= seg[:, None], axis=1, dtype=jnp.int32)
    starts, ends = own_part(starts_all), own_part(ends_all)

    attended_t, lse = attention_forward(q, k, vt, starts, ends, scale)
    attended_t, wd_near = tie(attended_t, wd_near)
    outgoing = attended_t.astype(BF).reshape(d, ctx, mine).transpose(1, 0, 2)
    incoming = lax.all_to_all(outgoing, "ctx", 0, 0, tiled=True)
    wd = assemble(w_down, wd_near, far_half(wd_near))
    incoming, wd = tie(incoming, wd)
    attended = incoming.reshape(heads, parts, d, mine).transpose(1, 3, 0, 2).reshape(block, width)
    branch = dot(attended, wo, 1, 0) + bo
    first, first_pull = jax.vjp(layer_norm, inputs.astype(F32) + branch, gain1, shift1)
    first_low = first.astype(BF)
    hidden_pre = dot(first_low, wu, 1, 0) + bu
    active, active_pull = jax.vjp(gelu_exact, hidden_pre)
    active_low = active.astype(BF)
    second = dot(active_low, wd, 1, 0) + bd
    output, out_pull = jax.vjp(layer_norm, first + second, gain2, shift2)

    d_second, grad_gain_two, grad_shift_two = out_pull(cotangent[0].astype(F32))
    d_second_low = d_second.astype(BF)
    core_step = ("ctx", 1)
    down_sent, down_keep, down_left = begin(active_low, d_second_low, core_step)
    down_sent, d_second_low = tie(down_sent, d_second_low)
    down_got = move(down_sent, core_step)
    (d_hidden,) = active_pull(dot(d_second_low, wd, 1, 1))
    d_hidden_low = d_hidden.astype(BF)
    up_sent, up_keep, up_left = begin(first_low, d_hidden_low, core_step)
    up_sent, d_hidden_low = tie(up_sent, d_hidden_low)
    up_got = move(up_sent, core_step)
    d_first = d_second + dot(d_hidden_low, wu, 1, 1)
    d_branch, grad_gain_one, grad_shift_one = first_pull(d_first)
    d_branch_low = d_branch.astype(BF)
    d_attended_t = dot(wo, d_branch_low, 1, 1).astype(BF)
    outgoing = d_attended_t.reshape(heads, d, parts, mine).transpose(0, 2, 1, 3).reshape(ctx, d, mine)
    do_t = lax.all_to_all(outgoing, "ctx", 0, 0, tiled=True)

    outgoing, down_left, up_left, attended = tie(outgoing, down_left, up_left, attended)
    place = [p for p in halves_of(None) if p != core_step]
    down = down_keep(down_left, down_got).reshape([2] * len(place) + [-1, width])
    rest = [("fsdp", b) for b in reversed(bits(fsdp))], [("ctx", b) for b in bits(ctx) if b > 1]
    down_order = rest[0] + rest[1]
    up_order = rest[1][:1] + rest[0] + rest[1][1:]
    down_place = up_place = place
    down_kept, down_send, down_place = split_step(down, down_place, down_order[0])
    down_got = move(down_send, down_order[0])
    out_sent, out_keep, out_left = begin(attended, d_branch_low, core_step)
    out_got = move(out_sent, core_step)
    up = up_keep(up_left, up_got)
    up = jnp.concatenate([up.reshape(-1, hidden), out_keep(out_left, out_got).reshape(-1, width)], axis=1)
    up = up.reshape([2] * len(place) + [-1, hidden + width])
    up_kept, up_send, up_place = split_step(up, up_place, up_order[0])
    up_got = move(up_send, up_order[0])
    do_t, down_send, up_send = tie(do_t, down_send, up_send)

    vectors = [
        jnp.sum(d_branch, axis=0), grad_gain_one, grad_shift_one, jnp.sum(d_second, axis=0), grad_gain_two,
        grad_shift_two,
    ]
    vectors = jnp.concatenate(
        [jnp.stack(vectors).reshape(6, fsdp, shard).transpose(1, 0, 2).reshape(fsdp, -1),
         jnp.sum(d_hidden, axis=0).reshape(fsdp, -1)], axis=1,
    )

    do = do_t.transpose(0, 2, 1).reshape(count, d)
    delta = jnp.sum(
        attended_t.reshape(d, ctx, mine) * do_t.transpose(1, 0, 2).astype(F32), axis=0
    ).reshape(1, count)
    bq, bk = min(512, count), 512
    ranges = block_ranges(starts_all, ends_all, bk, bq * parts)
    calls = 4
    blocks = length // bk // calls
    dqt = jnp.zeros((d, count), F32)
    dk, dv = [], []
    vector_steps = [("fsdp", b) for b in reversed(bits(fsdp))] + [("ctx", b) for b in bits(ctx)]
    todo = list(vector_steps)

    def vector_step(vectors, step):
        axis, bit = step
        if axis == "ctx":
            return vectors + flip(vectors, "ctx", bit, ctx)
        own = (row // bit) % 2
        pair = vectors.reshape(2, -1, vectors.shape[1])
        keep = lax.dynamic_index_in_dim(pair, own, 0, keepdims=False)
        return keep + flip(lax.dynamic_index_in_dim(pair, 1 - own, 0, keepdims=False), "fsdp", bit, fsdp)

    down_at, up_at = 1, 1
    for call in range(calls):
        dk_new, dv_new, dqt = attention_backward(
            q, k, v, kt, do, lse, delta, starts, ends, ranges, dqt, scale, bq, bk, call * blocks, blocks
        )
        dk.append(dk_new)
        dv.append(dv_new)
        if todo:
            vectors = vector_step(vectors, todo.pop(0))
        if call == calls - 2:
            down, up = add(down_kept, down_got), add(up_kept, up_got)
            down_kept, down_send, down_place = split_step(down, down_place, down_order[1])
            down_got = move(down_send, down_order[1])
            up_kept, up_send, up_place = split_step(up, up_place, up_order[1])
            up_got = move(up_send, up_order[1])
            dqt, down_send, up_send, vectors = tie(dqt, down_send, up_send, vectors)
            down_at, up_at = 2, 2
        elif call < calls - 1:
            dqt, vectors = tie(dqt, vectors)
    dk, dv = jnp.concatenate(dk), jnp.concatenate(dv)
    dq = (dqt.T * scale).astype(BF)

    share = lambda a: a.reshape(ctx, -1, d)
    wqkv_all = assemble(wqkv, wqkv_near, far_half(wqkv_near))
    wq, wk, wv = (wqkv_all[:, i * width : (i + 1) * width] for i in range(3))
    if parts == 1:
        outgoing = jnp.concatenate([dq, dk, dv], axis=1).reshape(ctx, block, 3 * d)
        incoming = lax.all_to_all(outgoing, "ctx", 0, 0, tiled=True)
        everyone_q = everyone
    else:
        back = lambda a: lax.all_to_all(share(a), "ctx", 0, 0, tiled=True).reshape(heads, parts, -1, d)
        dq_in = back(dq).transpose(1, 2, 0, 3).reshape(block, width)
        summed = lambda a: jnp.sum(back(a).astype(F32), axis=1).astype(BF).transpose(1, 0, 2).reshape(block, width)
        everyone_q = own_part(everyone)

    grad_head = jnp.concatenate([dot(everyone_q, dq, 0, 0), dot(everyone, dk, 0, 0), dot(everyone, dv, 0, 0)], axis=1)
    sums = jnp.concatenate(
        [jnp.sum(dq.astype(F32), axis=0), jnp.zeros((d,), F32), jnp.sum(dv.astype(F32), axis=0)]
    )
    sums = jnp.broadcast_to(sums[None, None], (fsdp, 16, 3 * d))
    grad_head = jnp.concatenate([grad_head.reshape(fsdp, shard, 3 * d), sums], axis=1)
    if fsdp == 2:
        sent = lax.dynamic_index_in_dim(grad_head, 1 - row, 0, keepdims=False).astype(BF)
        kept = lax.dynamic_index_in_dim(grad_head, row, 0, keepdims=False)
        grad_head = (kept + flip(sent, "fsdp", 1, 2).astype(F32)).astype(BF)
    else:
        grad_head = lax.psum_scatter(
            grad_head.reshape(-1, 3 * d).astype(BF), "fsdp", scatter_dimension=0, tiled=True
        )
    every = lax.all_gather(grad_head, "ctx", axis=0, tiled=False)

    down, up = add(down_kept, down_got), add(up_kept, up_got)
    while down_at < len(down_order):
        kept, send, down_place = split_step(down, down_place, down_order[down_at])
        down_got = move(send, down_order[down_at])
        up_kept, up_send, up_place = split_step(up, up_place, up_order[down_at])
        up_got = move(up_send, up_order[down_at])
        down, up = add(kept, down_got), add(up_kept, up_got)
        down_at += 1
    grad_w_down = spread(down, w_down.shape[0], width).astype(F32)
    grad_up_out = spread(up, shard, hidden + width)
    grad_w_up, grad_w_out = grad_up_out[:, :hidden].astype(F32), grad_up_out[:, hidden:].astype(F32)
    for step in todo:
        vectors = vector_step(vectors, step)
    six = vectors[0, : 6 * shard].reshape(6, shard)
    grad_b_up = vectors[0, 6 * shard :]

    if parts == 1:
        grads = [incoming[:, :, i * d : (i + 1) * d].transpose(1, 0, 2).reshape(block, width) for i in range(3)]
    else:
        grads = [dq_in, summed(dk), summed(dv)]
    token_grad = d_branch + dot(grads[0], wq, 1, 1) + dot(grads[1], wk, 1, 1) + dot(grads[2], wv, 1, 1)

    every = every.astype(F32).reshape(heads, parts, shard + 16, 3, d).sum(axis=1)
    every = every.transpose(2, 1, 0, 3).reshape(3, shard + 16, width)
    bias_q = cut(every[0, shard], row * shard, shard, 0)
    bias_v = cut(every[2, shard], row * shard, shard, 0)

    return (
        output[None].astype(BF),
        token_grad[None].astype(BF),
        every[0, :shard],
        every[1, :shard],
        every[2, :shard],
        grad_w_out,
        bias_q,
        bias_v,
        six[0],
        six[1],
        six[2],
        grad_w_up,
        grad_b_up,
        grad_w_down,
        six[3],
        six[4],
        six[5],
    )


def solution(mesh):
    line, matrix, rows = P("fsdp"), P("fsdp", None), P("fsdp", "ctx", None)
    placed = (
        (rows, matrix) + (matrix,) * 4 + (line,) * 5 + (matrix, line, matrix) + (line,) * 3 + (rows,)
    )
    outs = (rows, rows) + (matrix,) * 4 + (line,) * 5 + (matrix, line, matrix) + (line,) * 3
    return jax.shard_map(
        functools.partial(body, mesh.shape["ctx"], mesh.shape["fsdp"]),
        mesh=mesh,
        in_specs=placed,
        out_specs=outs,
        check_vma=False,
    )
```

time: 701 us -> 677 us (0.966)
  waiting for transfers between devices: 290 us -> 232 us
  other arithmetic: 38.7 us -> 56 us
  local copies, waits for them, and re-layouts: 142 us -> 152 us
  matrix products: 76.4 us -> 85.8 us
    ppermute x35 -> x27, waiting for transfers between devices: 284 us -> 232 us  [flip(): return lax.ppermute(value, axis, [(i, i ^ bit) for i in range(size)])]
    unnamed x106 -> x162, local copies, waits for them, and re-layouts: 24.9 us -> 41.6 us
    convert_element_type x4 -> x1, local copies, waits for them, and re-layouts: 16.1 us -> 6.65 us  [body(): grad_w_down = spread(down, w_down.shape[0], width).astype(F32)]
    dot_general x19, matrix products: 76.4 us -> 85.8 us  [dot(): lax.dot_general(left, right, (((on_left,), (on_right,)), ((), ())), prefe...]
    convert_element_type x14 -> x11, other arithmetic: 13 us -> 19.4 us  [the longest x8 13.3 us: add(): return (keep.astype(F32) + received.astype(F32)).astype(BF)]
    dynamic_update_slice x18 -> x12, local copies, waits for them, and re-layouts: 28.1 us -> 21.8 us  [the longest x4 8.54 us: assemble(): lax.dynamic_update_slice_in_dim(whole, far, (1 - row) * rows + (1 - core)...]
    dynamic_slice x12 -> x10, local copies, waits for them, and re-layouts: 16.8 us -> 11.5 us  [body(): cut = lambda a, at, size, axis: lax.dynamic_slice_in_dim(a, at, size, axis)]
    ppermute x35 -> x27, starting transfers between devices: 28.8 us -> 26.1 us  [flip(): return lax.ppermute(value, axis, [(i, i ^ bit) for i in range(size)])]
  transfers between devices with their start and end apart: 43 -> 34, of which waited for: 21 -> 14; matrix products, arithmetic and copies ran while one was open for 28% -> 24% of each run, Pallas kernels for 11% -> 11%
where the time goes in v2:
time: 677 us; the launch traced here: 666 us
  waiting for transfers between devices  232 us (34%)
  local copies, waits for them, and re-layouts  152 us (22%)
  matrix products  85.8 us (13%)
  Pallas kernels  81 us (12%)
  other arithmetic  56 us (8%)
  starting transfers between devices  43.9 us (6%)
  between operations  15.5 us (2%)
    ppermute x27, waiting for transfers between devices, flip(): return lax.ppermute(value, axis, [(i, i ^ bit) for i in range(size)])  232 us
    dot_general x19, matrix products, dot(): lax.dot_general(left, right, (((on_left,), (on_right,)), ((), ())), prefe...  85.8 us
    pallas_call x4, Pallas kernels, attention_backward(): pl.pallas_call(functools.partial(backward_kernel, bq=bq, scale=scale, bas...  49.3 us
    unnamed x162, local copies, waits for them, and re-layouts  41.6 us
    pallas_call x1, Pallas kernels, attention_forward(): pl.pallas_call(functools.partial(forward_kernel, bk=bk, scale=scale), out...  31.7 us
    ppermute x27, starting transfers between devices, flip(): return lax.ppermute(value, axis, [(i, i ^ bit) for i in range(size)])  26.1 us
    reduce_sum x1, other arithmetic, body(): ends_all = jnp.sum(seg[None, :] <= seg[:, None], axis=1, dtype=jnp.int32)  15.5 us
  transfers between devices with their start and end apart: 34, of which 14 were waited for; matrix products, arithmetic and copies ran while one was open for 24% of the time, Pallas kernels for 11%

profile of v2, /device:TPU:0, one launch (start us, length us, event | category | flops | bytes accessed | tf_op | source)
XLA Modules:
  0.0 665.7 jit_solution(11069126000560620756)
XLA Ops:
  22.7 3.1 constant_dynamic-slice_fusion.11
  25.8 13.9 %collective-permute-done.3 = bf16[1,6144]{1,0:T(2,128)(2,1)S(1)} collective-permute-done((bf16[1,6144]{1,0:T(2,128)(2,1)S(1)}, bf16[1,6144]{1,0:T(2,128)(2,1)S(1)}, u32[]{:S(2)}, u32[]{:S(2)}) %collective-permute-start.3) | collective-permute-done | bytes 12320 | tf_op jit(solution)/shard_map/ppermute | solution.py:36
  41.8 15.5 %convert_reduce_fusion = (s32[4096]{0:T(1024)S(1)}, s32[4096]{0:T(1024)S(1)}) fusion(s32[4096]{0:T(1024)S(1)} %bitcast.310), kind=kLoop, calls=%fused_computation | loop fusion | flops 100655104 | bytes 49152 | tf_op jit(solution)/shard_map/reduce_sum | solution.py:304
  60.2 23.7 %collective-permute-done = bf16[256,4096]{1,0:T(8,128)(2,1)S(1)} collective-permute-done((bf16[256,4096]{1,0:T(8,128)(2,1)}, bf16[256,4096]{1,0:T(8,128)(2,1)S(1)}, u32[]{:S(2)}, u32[]{:S(2)}) %collective-permute-start) | collective-permute-done | bytes 2097184 | tf_op jit(solution)/shard_map/ppermute | solution.py:36
  83.9 4.4 broadcast_in_dim.45
  97.0 3.1 constant_dynamic-update-slice_fusion.15
  100.2 5.7 fusion.1
  111.4 31.7 %attention_forward.1 = (f32[64,4096]{1,0:T(8,128)S(1)}, f32[1,4096]{1,0:T(1,128)S(1)}) custom-call(s32[4]{0:T(128)S(1)} %get-tuple-element.211.lo_ref, s32[4]{0:T(128)S(1)} %get-tuple-element.210.hi_ref, s32[4]{0:T(128)S(1)} %get-tuple-element.209.in_lo_ref, s32[4]{0:T(128)S(1)} %get-tuple-element.208.in_hi_ref, bf16[4096,64]{1,0:T(8,128)(2,1)S(1)} %copy-done.4, ...), custom_call_target="tpu_custom_call" | custom-call | flops 4294967296 | bytes 4194304 | tf_op jit(solution)/shard_map/attention_forward/pallas_call | solution.py:88
  144.6 6.3 all-to-all-start
  153.9 3.4 copy-done.39
  172.6 16.0 %multiply_convert_fusion = (bf16[256,4096]{1,0:T(8,128)(2,1)}, f32[256,4096]{1,0:T(8,128)}, f32[256,4096]{1,0:T(8,128)}) fusion(f32[4096]{0:T(1024)S(1)} %bitcast.299, bf16[256,1024]{1,0:T(8,128)(2,1)} %fusion.43, bf16[1024,4096]{1,0:T(8,128)(2,1)} %constant_dynamic-update-slice_fusion.15), kind=kOutput, calls=%fused_computation.17 | convolution fusion | flops 2216689664 | bytes 19415040 | tf_op jit(solution)/shard_map/dot_general | solution.py:30
  188.6 4.4 reshape.310
  193.0 6.6 fusion.91
  210.2 3.4 convolution_convert_fusion.1
  215.4 7.4 %fusion.83 = (f32[4096]{0:T(1024)S(1)}, bf16[256,4096]{1,0:T(8,128)(2,1)S(1)}) fusion(f32[256,4096]{1,0:T(8,128)S(1)} %copy-done.68, f32[256,4096]{1,0:T(8,128)S(1)} %copy-done.69, bf16[256,1024]{1,0:T(8,128)(2,1)S(1)} %get-tuple-element.81, bf16[4096,1024]{1,0:T(8,128)(2,1)} %constant_dynamic-update-slice_fusion.12), kind=kOutput, calls=%fused_computation.263 | convolution fusion | flops 2163208192 | bytes 19415040 | tf_op jit(solution)/shard_map/dot_general | solution.py:30
  222.8 3.3 convolution_convert_fusion
  226.0 6.1 multiply_reduce_fusion
  236.1 6.1 all-to-all-start.1
  251.9 3.5 add_convert_fusion.1
  260.5 3.5 add_convert_fusion
  276.6 13.4 %attention_backward.4 = (bf16[1024,64]{1,0:T(8,128)(2,1)S(1)}, bf16[1024,64]{1,0:T(8,128)(2,1)S(1)}, f32[64,4096]{1,0:T(8,128)S(1)}) custom-call(s32[8]{0:T(128)S(1)} %get-tuple-element.205.lo_ref, s32[8]{0:T(128)S(1)} %get-tuple-element.204.hi_ref, s32[8]{0:T(128)S(1)} %get-tuple-element.203.in_lo_ref, s32[8]{0:T(128)S(1)} %get-tuple-element.202.in_hi_ref, ...), custom_call_target="tpu_custom_call" | custom-call | flops 10737418240 | bytes 6291456 | tf_op jit(solution)/shard_map/attention_backward/pallas_call | solution.py:157
  290.1 12.5 %attention_backward.5 = (bf16[1024,64]{1,0:T(8,128)(2,1)S(1)}, bf16[1024,64]{1,0:T(8,128)(2,1)S(1)}, f32[64,4096]{1,0:T(8,128)S(1)}) custom-call(s32[8]{0:T(128)S(1)} %get-tuple-element.205.lo_ref, s32[8]{0:T(128)S(1)} %get-tuple-element.204.hi_ref, s32[8]{0:T(128)S(1)} %get-tuple-element.203.in_lo_ref, s32[8]{0:T(128)S(1)} %get-tuple-element.202.in_hi_ref, ...), custom_call_target="tpu_custom_call" | custom-call | flops 10737418240 | bytes 6291456 | tf_op jit(solution)/shard_map/attention_backward/pallas_call | solution.py:157
  314.8 12.9 %attention_backward.6 = (bf16[1024,64]{1,0:T(8,128)(2,1)S(1)}, bf16[1024,64]{1,0:T(8,128)(2,1)S(1)}, f32[64,4096]{1,0:T(8,128)S(1)}) custom-call(s32[8]{0:T(128)S(1)} %get-tuple-element.205.lo_ref, s32[8]{0:T(128)S(1)} %get-tuple-element.204.hi_ref, s32[8]{0:T(128)S(1)} %get-tuple-element.203.in_lo_ref, s32[8]{0:T(128)S(1)} %get-tuple-element.202.in_hi_ref, ...), custom_call_target="tpu_custom_call" | custom-call | flops 10737418240 | bytes 6291456 | tf_op jit(solution)/shard_map/attention_backward/pallas_call | solution.py:157
  332.6 3.2 fusion.3
  337.5 3.7 fusion
  342.5 10.4 %attention_backward.7 = (bf16[1024,64]{1,0:T(8,128)(2,1)S(1)}, bf16[1024,64]{1,0:T(8,128)(2,1)S(1)}, f32[64,4096]{1,0:T(8,128)S(1)}) custom-call(s32[8]{0:T(128)S(1)} %get-tuple-element.205.lo_ref, s32[8]{0:T(128)S(1)} %get-tuple-element.204.hi_ref, s32[8]{0:T(128)S(1)} %get-tuple-element.203.in_lo_ref, s32[8]{0:T(128)S(1)} %get-tuple-element.202.in_hi_ref, ...), custom_call_target="tpu_custom_call" | custom-call | flops 10737418240 | bytes 6291456 | tf_op jit(solution)/shard_map/attention_backward/pallas_call | solution.py:157
  355.9 5.2 fusion.65
  362.1 5.0 fusion.63
  367.3 5.0 fusion.46
  373.3 7.7 %collective-permute-done.18 = bf16[528,192]{0,1:T(8,128)(2,1)S(1)} collective-permute-done((bf16[528,192]{0,1:T(8,128)(2,1)S(1)}, bf16[528,192]{0,1:T(8,128)(2,1)S(1)}, u32[]{:S(2)}, u32[]{:S(2)}) %collective-permute-start.18) | collective-permute-done | bytes 202784 | tf_op jit(solution)/shard_map/ppermute | solution.py:36
  383.7 25.8 %collective-permute-done.24 = bf16[2,2,128,1024]{3,2,1,0:T(8,128)(2,1)} collective-permute-done((bf16[2,2,128,1024]{3,2,1,0:T(8,128)(2,1)}, bf16[2,2,128,1024]{3,2,1,0:T(8,128)(2,1)}, u32[]{:S(2)}, u32[]{:S(2)}) %collective-permute-start.24) | collective-permute-done | bytes 1048608 | tf_op jit(solution)/shard_map/ppermute | solution.py:36
  414.1 25.9 %collective-permute-done.25 = bf16[2,128,1024]{2,1,0:T(8,128)(2,1)} collective-permute-done((bf16[2,128,1024]{2,1,0:T(8,128)(2,1)S(1)}, bf16[2,128,1024]{2,1,0:T(8,128)(2,1)}, u32[]{:S(2)}, u32[]{:S(2)}) %collective-permute-start.25) | collective-permute-done | bytes 524320 | tf_op jit(solution)/shard_map/ppermute | solution.py:36
  441.9 14.1 %collective-permute-done.26 = bf16[128,1024]{1,0:T(8,128)(2,1)} collective-permute-done((bf16[128,1024]{1,0:T(8,128)(2,1)S(1)}, bf16[128,1024]{1,0:T(8,128)(2,1)}, u32[]{:S(2)}, u32[]{:S(2)}) %collective-permute-start.26) | collective-permute-done | bytes 262176 | tf_op jit(solution)/shard_map/ppermute | solution.py:36
  459.2 29.6 %collective-permute-done.19 = bf16[2,2,32,5120]{3,2,1,0:T(8,128)(2,1)S(1)} collective-permute-done((bf16[2,2,32,5120]{3,2,1,0:T(8,128)(2,1)}, bf16[2,2,32,5120]{3,2,1,0:T(8,128)(2,1)S(1)}, u32[]{:S(2)}, u32[]{:S(2)}) %collective-permute-start.19) | collective-permute-done | bytes 1310752 | tf_op jit(solution)/shard_map/ppermute | solution.py:36
  489.2 27.4 %collective-permute-done.20 = bf16[2,32,5120]{2,1,0:T(8,128)(2,1)S(1)} collective-permute-done((bf16[2,32,5120]{2,1,0:T(8,128)(2,1)S(1)}, bf16[2,32,5120]{2,1,0:T(8,128)(2,1)S(1)}, u32[]{:S(2)}, u32[]{:S(2)}) %collective-permute-start.20) | collective-permute-done | bytes 655392 | tf_op jit(solution)/shard_map/ppermute | solution.py:36
  519.2 14.8 %collective-permute-done.21 = bf16[32,5120]{1,0:T(8,128)(2,1)S(1)} collective-permute-done((bf16[32,5120]{1,0:T(8,128)(2,1)S(1)}, bf16[32,5120]{1,0:T(8,128)(2,1)S(1)}, u32[]{:S(2)}, u32[]{:S(2)}) %collective-permute-start.21) | collective-permute-done | bytes 327712 | tf_op jit(solution)/shard_map/ppermute | solution.py:36
  541.8 6.7 %maximum_maximum_fusion = bf16[4096,192]{0,1:T(8,128)(2,1)S(1)} fusion(bf16[1024,64]{0,1:T(8,128)(2,1)S(1)} %copy.149, bf16[1024,64]{0,1:T(8,128)(2,1)S(1)} %copy-done.51, bf16[1024,64]{0,1:T(8,128)(2,1)S(1)} %copy-done.49, bf16[1024,64]{0,1:T(8,128)(2,1)S(1)} %copy-done.50, bf16[1024,64]{0,1:T(8,128)(2,1)S(1)} %copy-done.61, ...), kind=kLoop, calls=%fused_computation.49 | loop fusion | flops 14155776 | bytes 3145728 | tf_op jit(solution)/shard_map/concatenate | solution.py:416
  549.8 5.1 all-to-all-start.2
  555.0 21.9 %collective-permute-done.16 = bf16[256,3072]{1,0:T(8,128)(2,1)} collective-permute-done((bf16[256,3072]{1,0:T(8,128)(2,1)}, bf16[256,3072]{1,0:T(8,128)(2,1)}, u32[]{:S(2)}, u32[]{:S(2)}) %collective-permute-start.16) | collective-permute-done | bytes 1572896 | tf_op jit(solution)/shard_map/ppermute | solution.py:36
  576.9 3.5 broadcast_in_dim.53
  584.9 13.6 %collective-permute-done.22 = f32[1,5120]{1,0:T(1,128)S(1)} collective-permute-done((f32[1,5120]{1,0:T(1,128)S(1)}, f32[1,5120]{1,0:T(1,128)S(1)}, u32[]{:S(2)}, u32[]{:S(2)}) %collective-permute-start.22) | collective-permute-done | bytes 20512 | tf_op jit(solution)/shard_map/ppermute | solution.py:36
  598.6 4.0 collective-permute-start.23
  603.9 10.7 %collective-permute-done.23 = f32[1,5120]{1,0:T(1,128)S(1)} collective-permute-done((f32[1,5120]{1,0:T(1,128)S(1)}, f32[1,5120]{1,0:T(1,128)S(1)}, u32[]{:S(2)}, u32[]{:S(2)}) %collective-permute-start.23) | collective-permute-done | bytes 20512 | tf_op jit(solution)/shard_map/ppermute | solution.py:36
  622.1 3.3 fusion.36
  625.4 3.1 copy.152
  628.5 3.3 slice_bitcast_fusion
  643.3 6.7 copy.154
  654.5 4.5 slice_convert_fusion
  (358 shorter events, 176.1 us)
Async XLA Ops:
  7.2 93.0 %all-gather.9.cloned.1.call-start = ((), (), s32[]{:S(2)}) async-start(), calls=%async_computation.3 | async-start | bytes 8912896 | tf_op jit(solution)/shard_map/all_gather | solution.py:276
  15.8 26.1 %copy-start.67 = (s32[1,4096]{1,0:T(1,128)S(1)}, s32[1,4096]{1,0:T(1,128)}, u32[]{:S(2)}) copy-start(s32[1,4096]{1,0:T(1,128)} %param.19) | copy-start | bytes 49156
  17.7 40.1 %copy-start.48 = (bf16[512,1024]{1,0:T(8,128)(2,1)S(1)}, bf16[512,1024]{1,0:T(8,128)(2,1)}, u32[]{:S(2)}) copy-start(bf16[512,1024]{1,0:T(8,128)(2,1)} %param.23) | copy-start | bytes 3145732
  17.7 24.1 %collective-permute-start.1 = (bf16[256,1024]{1,0:T(8,128)(2,1)}, bf16[256,1024]{1,0:T(8,128)(2,1)}, u32[]{:S(2)}, u32[]{:S(2)}) collective-permute-start(bf16[256,1024]{1,0:T(8,128)(2,1)} %constant_dynamic-slice_fusion.10), channel_id=1, source_target_pairs={{0,1},{1,0},{2,3},{3,2},{4,5},{5,4},{6,7},{7,6},{8,9},{9,8},{10,11... | collective-permute-start | bytes 1572872 | tf_op jit(solution)/shard_map/ppermute | solution.py:36
  20.7 19.3 %collective-permute-start.2 = (bf16[512,192]{1,0:T(8,128)(2,1)S(1)}, bf16[512,192]{1,0:T(8,128)(2,1)}, u32[]{:S(2)}, u32[]{:S(2)}) collective-permute-start(bf16[512,192]{1,0:T(8,128)(2,1)S(1)} %pad_maximum_fusion.4), channel_id=1, source_target_pairs={{0,1},{1,0},{2,3},{3,2},{4,5},{5,4},{6,7},{7,6},{8,9},{9,8},{10,11... | collective-permute-start | bytes 589832 | tf_op jit(solution)/shard_map/ppermute | solution.py:36
  20.7 19.1 %collective-permute-start.3 = (bf16[1,6144]{1,0:T(2,128)(2,1)S(1)}, bf16[1,6144]{1,0:T(2,128)(2,1)S(1)}, u32[]{:S(2)}, u32[]{:S(2)}) collective-permute-start(bf16[1,6144]{1,0:T(2,128)(2,1)S(1)} %broadcast_in_dim.44), channel_id=1, source_target_pairs={{0,1},{1,0},{2,3},{3,2},{4,5},{5,4},{6,7},{7,6},{8,9},{9,8},{10,11... | collective-permute-start | bytes 36872 | tf_op jit(solution)/shard_map/ppermute | solution.py:36
  25.8 58.1 %collective-permute-start = (bf16[256,4096]{1,0:T(8,128)(2,1)}, bf16[256,4096]{1,0:T(8,128)(2,1)S(1)}, u32[]{:S(2)}, u32[]{:S(2)}) collective-permute-start(bf16[256,4096]{1,0:T(8,128)(2,1)} %constant_dynamic-slice_fusion.11), channel_id=1, source_target_pairs={{0,1},{1,0},{2,3},{3,2},{4,5},{5,4},{6,7},{7,6},{8,9},{9,8},{10,11... | collective-permute-start | bytes 6291464 | tf_op jit(solution)/shard_map/ppermute | solution.py:36
  41.8 17.2 %collective-permute-start.4 = (bf16[256,1024]{1,0:T(8,128)(2,1)}, bf16[256,1024]{1,0:T(8,128)(2,1)}, u32[]{:S(2)}, u32[]{:S(2)}) collective-permute-start(bf16[256,1024]{1,0:T(8,128)(2,1)} %collective-permute-done.1), channel_id=1, source_target_pairs={{0,2},{2,0},{4,6},{6,4},{8,10},{10,8},{12,14},{14,12},{16,18},{18,... | collective-permute-start | bytes 1572872 | tf_op jit(solution)/shard_map/ppermute | solution.py:36
  60.1 23.7 %copy-start.36 = (bf16[1024,1024]{1,0:T(8,128)(2,1)}, bf16[1024,1024]{1,0:T(8,128)(2,1)S(1)}, u32[]{:S(2)}) copy-start(bf16[1024,1024]{1,0:T(8,128)(2,1)S(1)} %constant_dynamic-update-slice_fusion.17) | copy-start | bytes 6291460
  83.9 13.2 %collective-permute-start.5 = (bf16[256,4096]{1,0:T(8,128)(2,1)S(1)}, bf16[256,4096]{1,0:T(8,128)(2,1)}, u32[]{:S(2)}, u32[]{:S(2)}) collective-permute-start(bf16[256,4096]{1,0:T(8,128)(2,1)S(1)} %collective-permute-done), channel_id=1, source_target_pairs={{0,2},{2,0},{4,6},{6,4},{8,10},{10,8},{12,14},{14,12},{16,18},{18,... | collective-permute-start | bytes 6291464 | tf_op jit(solution)/shard_map/ppermute | solution.py:36
  93.6 49.6 %collective-permute-start.6 = (bf16[1024,1024]{1,0:T(8,128)(2,1)}, bf16[1024,1024]{1,0:T(8,128)(2,1)}, u32[]{:S(2)}, u32[]{:S(2)}) collective-permute-start(bf16[1024,1024]{1,0:T(8,128)(2,1)} %constant_dynamic-slice_fusion.7), channel_id=1, source_target_pairs={{0,1},{1,0},{2,3},{3,2},{4,5},{5,4},{6,7},{7,6},{8,9},{9,8},{10,11... | collective-permute-start | bytes 6291464 | tf_op jit(solution)/shard_map/ppermute | solution.py:36
  108.0 35.1 %copy-start = (bf16[4096,64]{1,0:T(8,128)(2,1)}, bf16[4096,64]{1,0:T(8,128)(2,1)S(1)}, u32[]{:S(2)}) copy-start(bf16[4096,64]{1,0:T(8,128)(2,1)S(1)} %get-tuple-element.222.k_ref) | copy-start | bytes 1572868
  143.2 7.7 %copy-start.44 = (bf16[1,256,1024]{2,1,0:T(8,128)(2,1)S(1)}, bf16[1,256,1024]{2,1,0:T(8,128)(2,1)}, u32[]{:S(2)}) copy-start(bf16[1,256,1024]{2,1,0:T(8,128)(2,1)} %param.35) | copy-start | bytes 1572868
  143.2 19.5 %collective-permute-start.7 = (bf16[1024,1024]{1,0:T(8,128)(2,1)}, bf16[1024,1024]{1,0:T(8,128)(2,1)}, u32[]{:S(2)}, u32[]{:S(2)}) collective-permute-start(bf16[1024,1024]{1,0:T(8,128)(2,1)} %collective-permute-done.6), channel_id=1, source_target_pairs={{0,2},{2,0},{4,6},{6,4},{8,10},{10,8},{12,14},{14,12},{16,18},{18,... | collective-permute-start | bytes 6291464 | tf_op jit(solution)/shard_map/ppermute | solution.py:36
  144.6 21.2 %all-to-all-start = ((bf16[16,64,256]{2,1,0:T(8,128)(2,1)}), bf16[16,64,256]{2,1,0:T(8,128)(2,1)S(1)}, u32[]{:S(2)}, u32[]{:S(2)}) async-start(bf16[16,64,256]{2,1,0:T(8,128)(2,1)} %bitcast.275), calls=%async_computation | async-start | bytes 1048576 | tf_op jit(solution)/shard_map/all_to_all | solution.py:310
  193.0 7.5 %copy-start.45 = (bf16[1,256,1024]{2,1,0:T(8,128)(2,1)S(1)}, bf16[1,256,1024]{2,1,0:T(8,128)(2,1)}, u32[]{:S(2)}) copy-start(bf16[1,256,1024]{2,1,0:T(8,128)(2,1)} %param.35) | copy-start | bytes 1572868
  193.0 8.0 %copy-start.52 = (bf16[256,1024]{0,1:T(8,128)(2,1)S(1)}, bf16[256,1024]{0,1:T(8,128)(2,1)}, u32[]{:S(2)}) copy-start(bf16[256,1024]{0,1:T(8,128)(2,1)} %copy.135) | copy-start | bytes 1572868
  222.8 9.4 %copy-start.34 = (bf16[256,4096]{1,0:T(8,128)(2,1)}, bf16[256,4096]{1,0:T(8,128)(2,1)S(1)}, u32[]{:S(2)}) copy-start(bf16[256,4096]{1,0:T(8,128)(2,1)S(1)} %get-tuple-element.82) | copy-start | bytes 6291460
  232.2 19.6 %collective-permute-start.8 = (bf16[2048,1024]{1,0:T(8,128)(2,1)}, bf16[2048,1024]{1,0:T(8,128)(2,1)}, u32[]{:S(2)}, u32[]{:S(2)}) collective-permute-start(bf16[2048,1024]{1,0:T(8,128)(2,1)} %convolution_convert_fusion.1), channel_id=1, source_target_pairs={{0,2},{2,0},{4,6},{6,4},{8,10},{10,8},{12,14},{14,12},{16,18},{18,... | collective-permute-start | bytes 12582920 | tf_op jit(solution)/shard_map/ppermute | solution.py:36
  232.8 27.7 %collective-permute-start.9 = (bf16[512,4096]{1,0:T(8,128)(2,1)}, bf16[512,4096]{1,0:T(8,128)(2,1)}, u32[]{:S(2)}, u32[]{:S(2)}) collective-permute-start(bf16[512,4096]{1,0:T(8,128)(2,1)} %convolution_convert_fusion), channel_id=1, source_target_pairs={{0,2},{2,0},{4,6},{6,4},{8,10},{10,8},{12,14},{14,12},{16,18},{18,... | collective-permute-start | bytes 12582920 | tf_op jit(solution)/shard_map/ppermute | solution.py:36
  234.4 7.8 %copy-start.46 = (bf16[256,1024]{1,0:T(8,128)(2,1)}, bf16[256,1024]{1,0:T(8,128)(2,1)S(1)}, u32[]{:S(2)}) copy-start(bf16[256,1024]{1,0:T(8,128)(2,1)S(1)} %get-tuple-element.231) | copy-start | bytes 1572868
  236.1 34.2 %all-to-all-start.1 = ((bf16[16,64,256]{2,1,0:T(8,128)(2,1)}), bf16[16,64,256]{2,1,0:T(8,128)(2,1)}, u32[]{:S(2)}, u32[]{:S(2)}) async-start(bf16[16,64,256]{2,1,0:T(8,128)(2,1)} %bitcast.19), calls=%async_computation.1 | async-start | bytes 1048576 | tf_op jit(solution)/shard_map/all_to_all | solution.py:339
  242.1 383.2 %all-gather.15.cloned.1.call-start = ((), (), s32[]{:S(2)}) async-start(), calls=%async_computation.6 | async-start | bytes 4177920 | tf_op jit(solution)/shard_map/all_gather | solution.py:439
  244.5 3.8 collective-permute-start.11
  247.6 2.7 collective-permute-start.10
  259.0 73.6 %collective-permute-start.13 = (bf16[2,2,2,128,1024]{4,3,2,1,0:T(8,128)(2,1)}, bf16[2,2,2,128,1024]{4,3,2,1,0:T(8,128)(2,1)}, u32[]{:S(2)}, u32[]{:S(2)}) collective-permute-start(bf16[2,2,2,128,1024]{4,3,2,1,0:T(8,128)(2,1)} %dynamic-slice_bitcast_fusion.1), channel_id=1, source_target_pairs={{0,1},{1,0},{2,3},{3,2},{4,5},{5,4},{6,7},{7,6},{8,9},{9,8},{10,11... | collective-permute-start | bytes 6291464 | tf_op jit(solution)/shard_map/ppermute | solution.py:36
  268.4 69.1 %collective-permute-start.14 = (bf16[2,2,2,32,5120]{4,3,2,1,0:T(8,128)(2,1)}, bf16[2,2,2,32,5120]{4,3,2,1,0:T(8,128)(2,1)}, u32[]{:S(2)}, u32[]{:S(2)}) collective-permute-start(bf16[2,2,2,32,5120]{4,3,2,1,0:T(8,128)(2,1)} %dynamic-slice_bitcast_fusion), channel_id=1, source_target_pairs={{0,4},{2,6},{4,0},{6,2},{8,12},{10,14},{12,8},{14,10},{16,20},{18,... | collective-permute-start | bytes 7864328 | tf_op jit(solution)/shard_map/ppermute | solution.py:36
  276.6 13.5 %copy-start.9 = (bf16[64,4096]{1,0:T(8,128)(2,1)S(1)}, bf16[64,4096]{1,0:T(8,128)(2,1)}, u32[]{:S(2)}) copy-start(bf16[64,4096]{1,0:T(8,128)(2,1)} %copy.141.kt_ref) | copy-start | bytes 1572868
  290.0 12.7 %copy-start.14 = (bf16[1024,64]{1,0:T(8,128)(2,1)}, bf16[1024,64]{1,0:T(8,128)(2,1)S(1)}, u32[]{:S(2)}) copy-start(bf16[1024,64]{1,0:T(8,128)(2,1)S(1)} %get-tuple-element.103) | copy-start | bytes 393220
  290.0 21.3 %copy-start.2 = (bf16[4096,64]{1,0:T(8,128)(2,1)S(1)}, bf16[4096,64]{1,0:T(8,128)(2,1)}, u32[]{:S(2)}) copy-start(bf16[4096,64]{1,0:T(8,128)(2,1)} %copy-done) | copy-start | bytes 1572868
  290.0 21.0 %collective-permute-start.12 = (f32[1,5120]{1,0:T(1,128)S(1)}, f32[1,5120]{1,0:T(1,128)S(1)}, u32[]{:S(2)}, u32[]{:S(2)}) collective-permute-start(f32[1,5120]{1,0:T(1,128)S(1)} %fusion.68), channel_id=1, source_target_pairs={{0,2},{2,0},{4,6},{6,4},{8,10},{10,8},{12,14},{14,12},{16,18},{18,... | collective-permute-start | bytes 61448 | tf_op jit(solution)/shard_map/ppermute | solution.py:36
  311.1 20.9 %collective-permute-start.15 = (f32[1,5120]{1,0:T(1,128)S(1)}, f32[1,5120]{1,0:T(1,128)S(1)}, u32[]{:S(2)}, u32[]{:S(2)}) collective-permute-start(f32[1,5120]{1,0:T(1,128)S(1)} %add.377), channel_id=1, source_target_pairs={{0,4},{2,6},{4,0},{6,2},{8,12},{10,14},{12,8},{14,10},{16,20},{18,... | collective-permute-start | bytes 61448 | tf_op jit(solution)/shard_map/ppermute | solution.py:36
  341.2 11.8 %copy-start.25 = (bf16[2,2,2,32,5120]{4,3,2,1,0:T(8,128)(2,1)}, bf16[2,2,2,32,5120]{4,3,2,1,0:T(8,128)(2,1)S(1)}, u32[]{:S(2)}) copy-start(bf16[2,2,2,32,5120]{4,3,2,1,0:T(8,128)(2,1)S(1)} %fusion) | copy-start | bytes 7864324
  372.7 8.3 %collective-permute-start.18 = (bf16[528,192]{0,1:T(8,128)(2,1)S(1)}, bf16[528,192]{0,1:T(8,128)(2,1)S(1)}, u32[]{:S(2)}, u32[]{:S(2)}) collective-permute-start(bf16[528,192]{0,1:T(8,128)(2,1)S(1)} %fusion.62), channel_id=1, source_target_pairs={{0,1},{1,0},{2,3},{3,2},{4,5},{5,4},{6,7},{7,6},{8,9},{9,8},{10,11... | collective-permute-start | bytes 608264 | tf_op jit(solution)/shard_map/ppermute | solution.py:36
  381.7 107.1 %copy-start.26 = (bf16[2,2,2,32,5120]{4,3,2,1,0:T(8,128)(2,1)S(1)}, bf16[2,2,2,32,5120]{4,3,2,1,0:T(8,128)(2,1)}, u32[]{:S(2)}) copy-start(bf16[2,2,2,32,5120]{4,3,2,1,0:T(8,128)(2,1)} %copy-done.25) | copy-start | bytes 7864324
  381.7 261.6 %all-gather.13.cloned.1.call-start = ((), (), s32[]{:S(2)}) async-start(), calls=%async_computation.5 | async-start | bytes 4456448 | tf_op jit(solution)/shard_map/all_gather | solution.py:265
  381.9 27.6 %collective-permute-start.24 = (bf16[2,2,128,1024]{3,2,1,0:T(8,128)(2,1)}, bf16[2,2,128,1024]{3,2,1,0:T(8,128)(2,1)}, u32[]{:S(2)}, u32[]{:S(2)}) collective-permute-start(bf16[2,2,128,1024]{3,2,1,0:T(8,128)(2,1)} %dynamic-slice_bitcast_fusion.3), channel_id=1, source_target_pairs={{0,4},{2,6},{4,0},{6,2},{8,12},{10,14},{12,8},{14,10},{16,20},{18,... | collective-permute-start | bytes 3145736 | tf_op jit(solution)/shard_map/ppermute | solution.py:36
  412.6 27.5 %collective-permute-start.25 = (bf16[2,128,1024]{2,1,0:T(8,128)(2,1)S(1)}, bf16[2,128,1024]{2,1,0:T(8,128)(2,1)}, u32[]{:S(2)}, u32[]{:S(2)}) collective-permute-start(bf16[2,128,1024]{2,1,0:T(8,128)(2,1)S(1)} %dynamic-slice_bitcast_fusion.5), channel_id=1, source_target_pairs={{0,8},{2,10},{4,12},{6,14},{8,0},{10,2},{12,4},{14,6},{16,24},{18,... | collective-permute-start | bytes 1572872 | tf_op jit(solution)/shard_map/ppermute | solution.py:36
  441.5 14.5 %collective-permute-start.26 = (bf16[128,1024]{1,0:T(8,128)(2,1)S(1)}, bf16[128,1024]{1,0:T(8,128)(2,1)}, u32[]{:S(2)}, u32[]{:S(2)}) collective-permute-start(bf16[128,1024]{1,0:T(8,128)(2,1)S(1)} %dynamic-slice_bitcast_fusion.7), channel_id=1, source_target_pairs={{0,16},{2,18},{4,20},{6,22},{8,24},{10,26},{12,28},{14,30},{16,0},... | collective-permute-start | bytes 786440 | tf_op jit(solution)/shard_map/ppermute | solution.py:36
  457.7 192.2 %all-gather.11.cloned.1.call-start = ((), (), s32[]{:S(2)}) async-start(), calls=%async_computation.4 | async-start | bytes 5570560 | tf_op jit(solution)/shard_map/all_gather | solution.py:265
  457.8 31.0 %collective-permute-start.19 = (bf16[2,2,32,5120]{3,2,1,0:T(8,128)(2,1)}, bf16[2,2,32,5120]{3,2,1,0:T(8,128)(2,1)S(1)}, u32[]{:S(2)}, u32[]{:S(2)}) collective-permute-start(bf16[2,2,32,5120]{3,2,1,0:T(8,128)(2,1)} %dynamic-slice_bitcast_fusion.2), channel_id=1, source_target_pairs={{0,1},{1,0},{2,3},{3,2},{4,5},{5,4},{6,7},{7,6},{8,9},{9,8},{10,11... | collective-permute-start | bytes 3932168 | tf_op jit(solution)/shard_map/ppermute | solution.py:36
  489.1 27.4 %collective-permute-start.20 = (bf16[2,32,5120]{2,1,0:T(8,128)(2,1)S(1)}, bf16[2,32,5120]{2,1,0:T(8,128)(2,1)S(1)}, u32[]{:S(2)}, u32[]{:S(2)}) collective-permute-start(bf16[2,32,5120]{2,1,0:T(8,128)(2,1)S(1)} %dynamic-slice_bitcast_fusion.4), channel_id=1, source_target_pairs={{0,8},{2,10},{4,12},{6,14},{8,0},{10,2},{12,4},{14,6},{16,24},{18,... | collective-permute-start | bytes 1966088 | tf_op jit(solution)/shard_map/ppermute | solution.py:36
  516.8 17.3 %collective-permute-start.21 = (bf16[32,5120]{1,0:T(8,128)(2,1)S(1)}, bf16[32,5120]{1,0:T(8,128)(2,1)S(1)}, u32[]{:S(2)}, u32[]{:S(2)}) collective-permute-start(bf16[32,5120]{1,0:T(8,128)(2,1)S(1)} %dynamic-slice_bitcast_fusion.6), channel_id=1, source_target_pairs={{0,16},{2,18},{4,20},{6,22},{8,24},{10,26},{12,28},{14,30},{16,0},... | collective-permute-start | bytes 983048 | tf_op jit(solution)/shard_map/ppermute | solution.py:36
  540.2 36.6 %collective-permute-start.16 = (bf16[256,3072]{1,0:T(8,128)(2,1)}, bf16[256,3072]{1,0:T(8,128)(2,1)}, u32[]{:S(2)}, u32[]{:S(2)}) collective-permute-start(bf16[256,3072]{1,0:T(8,128)(2,1)} %constant_dynamic-slice_fusion), channel_id=1, source_target_pairs={{0,1},{1,0},{2,3},{3,2},{4,5},{5,4},{6,7},{7,6},{8,9},{9,8},{10,11... | collective-permute-start | bytes 4718600 | tf_op jit(solution)/shard_map/ppermute | solution.py:36
  549.8 66.0 %all-to-all-start.2 = ((bf16[16,256,192]{1,2,0:T(8,128)(2,1)}), bf16[16,256,192]{1,2,0:T(8,128)(2,1)}, u32[]{:S(2)}, u32[]{:S(2)}) async-start(bf16[16,256,192]{1,2,0:T(8,128)(2,1)} %bitcast.263), calls=%async_computation.2 | async-start | bytes 3145728 | tf_op jit(solution)/shard_map/all_to_all | solution.py:417
  576.9 25.7 %collective-permute-start.17 = (bf16[256,3072]{1,0:T(8,128)(2,1)}, bf16[256,3072]{1,0:T(8,128)(2,1)S(1)}, u32[]{:S(2)}, u32[]{:S(2)}) collective-permute-start(bf16[256,3072]{1,0:T(8,128)(2,1)} %collective-permute-done.16), channel_id=1, source_target_pairs={{0,2},{2,0},{4,6},{6,4},{8,10},{10,8},{12,14},{14,12},{16,18},{18,... | collective-permute-start | bytes 4718600 | tf_op jit(solution)/shard_map/ppermute | solution.py:36
  582.2 16.3 %collective-permute-start.22 = (f32[1,5120]{1,0:T(1,128)S(1)}, f32[1,5120]{1,0:T(1,128)S(1)}, u32[]{:S(2)}, u32[]{:S(2)}) collective-permute-start(f32[1,5120]{1,0:T(1,128)S(1)} %copy-done.64), channel_id=1, source_target_pairs={{0,8},{2,10},{4,12},{6,14},{8,0},{10,2},{12,4},{14,6},{16,24},{18,... | collective-permute-start | bytes 61448 | tf_op jit(solution)/shard_map/ppermute | solution.py:36
  598.6 16.0 %collective-permute-start.23 = (f32[1,5120]{1,0:T(1,128)S(1)}, f32[1,5120]{1,0:T(1,128)S(1)}, u32[]{:S(2)}, u32[]{:S(2)}) collective-permute-start(f32[1,5120]{1,0:T(1,128)S(1)} %add.397), channel_id=1, source_target_pairs={{0,16},{2,18},{4,20},{6,22},{8,24},{10,26},{12,28},{14,30},{16,0},... | collective-permute-start | bytes 61448 | tf_op jit(solution)/shard_map/ppermute | solution.py:36
  (56 other events, 187.8 us)
Sparse Core Ops, SparseCore 0:
  15.9 77.1 all-gather.8
  381.8 57.6 all-gather.14
  457.9 53.7 all-gather.12
  535.0 76.0 all-gather.10
